TPU v7x, 512 devices: a whole 4x4x16 slice. The times are simulated.
512 devices in a mesh: dp: 8 (over z_lo), seq: 64 (over x, z_hi, y, core).
Axes of the slice: x: 4, y: 4, z: 16 (z_hi: 2, z_lo: 8; z = z_hi * 8 + z_lo), core: 2. Of those that a mesh axis runs over, the one named last changes fastest.
Arguments:
- queries: bfloat16 [8, 8192, 2048], P('dp', 'seq'), may hold values from -60 to 60
- raw_key_rows: bfloat16 [8, 8192, 1024], P('dp', 'seq'), may hold values from -60 to 60
- values: bfloat16 [8, 8192, 1024], P('dp', 'seq'), may hold values from -6 to 6
- out_grad: bfloat16 [8, 8192, 2048], P('dp', 'seq'), may hold values from -96 to 96
- query_gain: float32 [128], P('dp'), may hold values from 0.5 to 6
- key_norm_gain: float32 [128], P('dp'), may hold values from 0.5 to 6
Outputs:
- query_grad: bfloat16 [8, 8192, 2048], P('dp', 'seq')
- key_gradient: bfloat16 [8, 8192, 1024], P('dp', 'seq')
- value_gradient: bfloat16 [8, 8192, 1024], P('dp', 'seq')
All inputs are finite; a program needn't handle non-finite values.
Results may differ from a plain program's by a relative error of at most 0.04.
The roundings to bfloat16 on the way count: a program that leaves them out, or rounds other values in their place, can miss the bound.
Values may be sent and summed in bfloat16 or wider, within the bound.
A program may use at most 64 MiB of HBM per device.

v0:
```python
import jax
import jax.numpy as jnp
from jax import lax
from jax.sharding import PartitionSpec as P

QUERY_HEADS = 16
KEY_VALUE_HEADS = 8
HEAD_SIZE = 128
WINDOW_KEYS = 1024


SCALE = 168.0 ** (-0.5)
ROPE_BASE = 10000.0
EPSILON = 1e-06


def passed_along(block, axis, distance):
    devices = range(lax.axis_size(axis))
    route = [(i - distance, i) for i in devices if i - distance in devices]
    return lax.ppermute(block, axis, route)


def prepare_inputs(input_arrays, gain, token_positions):
    depth = input_arrays.shape[-1]
    half_depth = depth // 2
    inverse = lax.rsqrt(jnp.mean(input_arrays * input_arrays, axis=-1, keepdims=True) + EPSILON)
    normed = input_arrays * inverse * gain
    frequency = ROPE_BASE ** (-jnp.arange(half_depth).astype(input_arrays.dtype) * (2.0 / depth))
    angles = token_positions.astype(input_arrays.dtype)[:, None] * frequency[None, :]
    cosine = jnp.cos(angles)[:, None, :]
    sine_val = jnp.sin(angles)[:, None, :]
    first_half = normed[..., :half_depth]
    second_half = normed[..., half_depth:]
    return jnp.concatenate(
        [
            first_half * cosine - second_half * sine_val,
            second_half * cosine + first_half * sine_val,
        ],
        axis=-1,
    )


def visible(anchor, row_list, span):
    query_pos = anchor + jnp.arange(row_list, dtype=jnp.int32)
    key_pos = anchor - WINDOW_KEYS + jnp.arange(span, dtype=jnp.int32)
    return (
        (key_pos[None, :] >= 0)
        & (key_pos[None, :] > query_pos[:, None] - WINDOW_KEYS)
        & (key_pos[None, :] <= query_pos[:, None])
    )


def attend_head(operands, mask_table):
    query_group, key_block, value_block, grad_group = operands
    scores = SCALE * jnp.einsum(
        "gtd,ld->gtl", query_group, key_block, preferred_element_type=jnp.float32
    )
    scores = jnp.where(mask_table[None], scores, -1e30)
    row_max = jnp.max(scores, axis=-1, keepdims=True)
    weights = jnp.exp(scores - row_max)
    probs = weights / jnp.sum(weights, axis=-1, keepdims=True)
    probs_b = probs.astype(jnp.bfloat16)
    attn_out = jnp.einsum("gtl,ld->gtd", probs_b, value_block, preferred_element_type=jnp.float32)
    dprob = jnp.einsum("gtd,ld->gtl", grad_group, value_block, preferred_element_type=jnp.float32)
    delta = jnp.sum(grad_group.astype(jnp.float32) * attn_out, axis=-1, keepdims=True)
    dscore_b = (probs * (dprob - delta)).astype(jnp.bfloat16)
    dq_part = SCALE * jnp.einsum(
        "gtl,ld->gtd", dscore_b, key_block, preferred_element_type=jnp.float32
    )
    dk_part = SCALE * jnp.einsum(
        "gtl,gtd->ld", dscore_b, query_group, preferred_element_type=jnp.float32
    )
    dv_part = jnp.einsum("gtl,gtd->ld", probs_b, grad_group, preferred_element_type=jnp.float32)
    return (dq_part, dk_part, dv_part)


def head_terms(query_tile, key_block, value_block, gradient_block, mask_table):
    row_list = query_tile.shape[0]
    group_width = QUERY_HEADS // KEY_VALUE_HEADS
    query_group_rows = query_tile.reshape(
        row_list, KEY_VALUE_HEADS, group_width, HEAD_SIZE
    ).transpose(1, 2, 0, 3)
    gradient_groups = gradient_block.reshape(
        row_list, KEY_VALUE_HEADS, group_width, HEAD_SIZE
    ).transpose(1, 2, 0, 3)
    key_heads = key_block.transpose(1, 0, 2)
    value_head_rows = value_block.transpose(1, 0, 2)
    dq_part, dk_part, dv_part = lax.map(
        lambda operands: attend_head(operands, mask_table),
        (query_group_rows, key_heads, value_head_rows, gradient_groups),
    )
    return (
        dq_part.transpose(2, 0, 1, 3).reshape(row_list, QUERY_HEADS, HEAD_SIZE),
        dk_part.transpose(1, 0, 2),
        dv_part.transpose(1, 0, 2),
    )


def body(queries, raw_key_rows, values, out_grad, query_gain, key_norm_gain):
    row_list = queries.shape[1]
    reach = WINDOW_KEYS // row_list
    gains = lax.all_gather(jnp.stack([query_gain, key_norm_gain]), "dp", axis=1, tiled=True)
    anchor = lax.axis_index("seq") * row_list
    token_positions = anchor + jnp.arange(row_list, dtype=jnp.int32)
    query_prep, query_back = jax.vjp(
        lambda input_arrays: prepare_inputs(input_arrays, gains[0], token_positions),
        queries[0].astype(jnp.float32).reshape(row_list, QUERY_HEADS, HEAD_SIZE),
    )
    key_prepared, key_backward = jax.vjp(
        lambda input_arrays: prepare_inputs(input_arrays, gains[1], token_positions),
        raw_key_rows[0].astype(jnp.float32).reshape(row_list, KEY_VALUE_HEADS, HEAD_SIZE),
    )
    query_hat = query_prep.astype(jnp.bfloat16)
    key_normalized = key_prepared.astype(jnp.bfloat16)
    grad_heads = out_grad[0].reshape(row_list, QUERY_HEADS, HEAD_SIZE)
    local_pair = jnp.stack(
        [key_normalized, values[0].reshape(row_list, KEY_VALUE_HEADS, HEAD_SIZE)]
    )
    arrived = []
    moving = local_pair
    for counter in range(reach):
        moving = passed_along(moving, "seq", 1)
        arrived.append(moving)
    joined = jnp.concatenate(arrived[::-1] + [local_pair], axis=1)
    mask_table = visible(anchor, row_list, WINDOW_KEYS + row_list)
    dq_hat, key_terms, value_terms = head_terms(
        query_hat, joined[0], joined[1], grad_heads, mask_table
    )
    terms = jnp.stack([key_terms, value_terms])
    remote_terms = terms[:, :WINDOW_KEYS].astype(jnp.bfloat16)
    incoming_terms = jnp.zeros((2, row_list, KEY_VALUE_HEADS, HEAD_SIZE), jnp.float32)
    for distance in range(reach, 0, -1):
        incoming_terms = passed_along(
            (
                incoming_terms
                + remote_terms[
                    :, (reach - distance) * row_list : (reach - distance + 1) * row_list
                ].astype(jnp.float32)
            ).astype(jnp.bfloat16),
            "seq",
            -1,
        ).astype(jnp.float32)
    local_terms = terms[:, WINDOW_KEYS:] + incoming_terms
    query_grad = (
        query_back(dq_hat)[0].astype(jnp.bfloat16).reshape(1, row_list, QUERY_HEADS * HEAD_SIZE)
    )
    key_gradient = (
        key_backward(local_terms[0])[0]
        .astype(jnp.bfloat16)
        .reshape(1, row_list, KEY_VALUE_HEADS * HEAD_SIZE)
    )
    value_gradient = (
        local_terms[1].astype(jnp.bfloat16).reshape(1, row_list, KEY_VALUE_HEADS * HEAD_SIZE)
    )
    return (query_grad, key_gradient, value_gradient)


def solution(mesh):
    return jax.shard_map(
        body,
        mesh=mesh,
        in_specs=(
            P("dp", "seq", None),
            P("dp", "seq", None),
            P("dp", "seq", None),
            P("dp", "seq", None),
            P("dp"),
            P("dp"),
        ),
        out_specs=(P("dp", "seq", None), P("dp", "seq", None), P("dp", "seq", None)),
        check_vma=False,
    )
```

profile of v0, /device:TPU:125, one launch (start us, length us, event | category | flops | bytes accessed | tf_op | source)
XLA Modules:
  0.0 622.4 jit_solution(12848671357032403875)
XLA Ops:
  1.4 15.2 %all-gather = f32[8,16,2]{1,2,0:T(2,128)S(1)} all-gather(f32[1,16,2]{1,2,0:T(2,128)S(1)} %maximum_bitcast_fusion.1), channel_id=1, replica_groups=mesh['dp'=8,'seq'=64] {'dp'}, dimensions={0}, use_global_device_ids=true | all-gather | bytes 1152 | tf_op jit(solution)/shard_map/all_gather | solution.py:102
  19.5 16.2 %collective-permute-start = (bf16[2,128,8,128]{1,3,2,0:T(8,128)(2,1)S(1)}, bf16[2,128,8,128]{1,3,2,0:T(8,128)(2,1)S(1)}, u32[]{:S(2)}, u32[]{:S(2)}) collective-permute-start(bf16[2,128,8,128]{1,3,2,0:T(8,128)(2,1)S(1)} %pad_maximum_fusion.1), channel_id=1, source_target_pairs={{0,1},{1,2},{2,3},{3,4},{4,5},{5,6},{6,7},{7,8},{8,9},{9,10},{10,1... | collective-permute-start | bytes 1572872 | tf_op jit(solution)/shard_map/ppermute | solution.py:20
  35.8 11.8 %collective-permute-done = bf16[2,128,8,128]{1,3,2,0:T(8,128)(2,1)S(1)} collective-permute-done((bf16[2,128,8,128]{1,3,2,0:T(8,128)(2,1)S(1)}, bf16[2,128,8,128]{1,3,2,0:T(8,128)(2,1)S(1)}, u32[]{:S(2)}, u32[]{:S(2)}) %collective-permute-start) | collective-permute-done | bytes 524320 | tf_op jit(solution)/shard_map/ppermute | solution.py:20
  47.6 26.4 %collective-permute-start.1 = (bf16[2,128,8,128]{1,3,2,0:T(8,128)(2,1)S(1)}, bf16[2,128,8,128]{1,3,2,0:T(8,128)(2,1)S(1)}, u32[]{:S(2)}, u32[]{:S(2)}) collective-permute-start(bf16[2,128,8,128]{1,3,2,0:T(8,128)(2,1)S(1)} %collective-permute-done), channel_id=1, source_target_pairs={{0,1},{1,2},{2,3},{3,4},{4,5},{5,6},{6,7},{7,8},{8,9},{9,10},{10,1... | collective-permute-start | bytes 1572872 | tf_op jit(solution)/shard_map/ppermute | solution.py:20
  74.0 22.8 %collective-permute-done.1 = bf16[2,128,8,128]{1,3,2,0:T(8,128)(2,1)S(1)} collective-permute-done((bf16[2,128,8,128]{1,3,2,0:T(8,128)(2,1)S(1)}, bf16[2,128,8,128]{1,3,2,0:T(8,128)(2,1)S(1)}, u32[]{:S(2)}, u32[]{:S(2)}) %collective-permute-start.1) | collective-permute-done | bytes 524320 | tf_op jit(solution)/shard_map/ppermute | solution.py:20
  96.8 15.3 %collective-permute-start.2 = (bf16[2,128,8,128]{1,3,2,0:T(8,128)(2,1)S(1)}, bf16[2,128,8,128]{1,3,2,0:T(8,128)(2,1)S(1)}, u32[]{:S(2)}, u32[]{:S(2)}) collective-permute-start(bf16[2,128,8,128]{1,3,2,0:T(8,128)(2,1)S(1)} %collective-permute-done.1), channel_id=1, source_target_pairs={{0,1},{1,2},{2,3},{3,4},{4,5},{5,6},{6,7},{7,8},{8,9},{9,10},{10,1... | collective-permute-start | bytes 1572872 | tf_op jit(solution)/shard_map/ppermute | solution.py:20
  112.1 16.1 %collective-permute-done.2 = bf16[2,128,8,128]{1,3,2,0:T(8,128)(2,1)S(1)} collective-permute-done((bf16[2,128,8,128]{1,3,2,0:T(8,128)(2,1)S(1)}, bf16[2,128,8,128]{1,3,2,0:T(8,128)(2,1)S(1)}, u32[]{:S(2)}, u32[]{:S(2)}) %collective-permute-start.2) | collective-permute-done | bytes 524320 | tf_op jit(solution)/shard_map/ppermute | solution.py:20
  128.3 32.1 %collective-permute-start.3 = (bf16[2,128,8,128]{1,3,2,0:T(8,128)(2,1)S(1)}, bf16[2,128,8,128]{1,3,2,0:T(8,128)(2,1)S(1)}, u32[]{:S(2)}, u32[]{:S(2)}) collective-permute-start(bf16[2,128,8,128]{1,3,2,0:T(8,128)(2,1)S(1)} %collective-permute-done.2), channel_id=1, source_target_pairs={{0,1},{1,2},{2,3},{3,4},{4,5},{5,6},{6,7},{7,8},{8,9},{9,10},{10,1... | collective-permute-start | bytes 1572872 | tf_op jit(solution)/shard_map/ppermute | solution.py:20
  160.4 21.7 %collective-permute-done.3 = bf16[2,128,8,128]{1,3,2,0:T(8,128)(2,1)S(1)} collective-permute-done((bf16[2,128,8,128]{1,3,2,0:T(8,128)(2,1)S(1)}, bf16[2,128,8,128]{1,3,2,0:T(8,128)(2,1)S(1)}, u32[]{:S(2)}, u32[]{:S(2)}) %collective-permute-start.3) | collective-permute-done | bytes 524320 | tf_op jit(solution)/shard_map/ppermute | solution.py:20
  182.0 15.4 %collective-permute-start.4 = (bf16[2,128,8,128]{1,3,2,0:T(8,128)(2,1)S(1)}, bf16[2,128,8,128]{1,3,2,0:T(8,128)(2,1)S(1)}, u32[]{:S(2)}, u32[]{:S(2)}) collective-permute-start(bf16[2,128,8,128]{1,3,2,0:T(8,128)(2,1)S(1)} %collective-permute-done.3), channel_id=1, source_target_pairs={{0,1},{1,2},{2,3},{3,4},{4,5},{5,6},{6,7},{7,8},{8,9},{9,10},{10,1... | collective-permute-start | bytes 1572872 | tf_op jit(solution)/shard_map/ppermute | solution.py:20
  197.4 12.7 %collective-permute-done.4 = bf16[2,128,8,128]{1,3,2,0:T(8,128)(2,1)S(1)} collective-permute-done((bf16[2,128,8,128]{1,3,2,0:T(8,128)(2,1)S(1)}, bf16[2,128,8,128]{1,3,2,0:T(8,128)(2,1)S(1)}, u32[]{:S(2)}, u32[]{:S(2)}) %collective-permute-start.4) | collective-permute-done | bytes 524320 | tf_op jit(solution)/shard_map/ppermute | solution.py:20
  210.2 15.3 %collective-permute-start.5 = (bf16[2,128,8,128]{1,3,2,0:T(8,128)(2,1)S(1)}, bf16[2,128,8,128]{1,3,2,0:T(8,128)(2,1)}, u32[]{:S(2)}, u32[]{:S(2)}) collective-permute-start(bf16[2,128,8,128]{1,3,2,0:T(8,128)(2,1)S(1)} %collective-permute-done.4), channel_id=1, source_target_pairs={{0,1},{1,2},{2,3},{3,4},{4,5},{5,6},{6,7},{7,8},{8,9},{9,10},{10,1... | collective-permute-start | bytes 1572872 | tf_op jit(solution)/shard_map/ppermute | solution.py:20
  225.8 10.8 %collective-permute-done.5 = bf16[2,128,8,128]{1,3,2,0:T(8,128)(2,1)} collective-permute-done((bf16[2,128,8,128]{1,3,2,0:T(8,128)(2,1)S(1)}, bf16[2,128,8,128]{1,3,2,0:T(8,128)(2,1)}, u32[]{:S(2)}, u32[]{:S(2)}) %collective-permute-start.5) | collective-permute-done | bytes 524320 | tf_op jit(solution)/shard_map/ppermute | solution.py:20
  236.6 15.4 %collective-permute-start.6 = (bf16[2,128,8,128]{1,3,2,0:T(8,128)(2,1)}, bf16[2,128,8,128]{1,3,2,0:T(8,128)(2,1)}, u32[]{:S(2)}, u32[]{:S(2)}) collective-permute-start(bf16[2,128,8,128]{1,3,2,0:T(8,128)(2,1)} %collective-permute-done.5), channel_id=1, source_target_pairs={{0,1},{1,2},{2,3},{3,4},{4,5},{5,6},{6,7},{7,8},{8,9},{9,10},{10,1... | collective-permute-start | bytes 1572872 | tf_op jit(solution)/shard_map/ppermute | solution.py:20
  253.1 6.1 collective-permute-done.6
  259.2 15.2 %collective-permute-start.7 = (bf16[2,128,8,128]{1,3,2,0:T(8,128)(2,1)}, bf16[2,128,8,128]{1,3,2,0:T(8,128)(2,1)}, u32[]{:S(2)}, u32[]{:S(2)}) collective-permute-start(bf16[2,128,8,128]{1,3,2,0:T(8,128)(2,1)} %collective-permute-done.6), channel_id=1, source_target_pairs={{0,1},{1,2},{2,3},{3,4},{4,5},{5,6},{6,7},{7,8},{8,9},{9,10},{10,1... | collective-permute-start | bytes 1572872 | tf_op jit(solution)/shard_map/ppermute | solution.py:20
  275.0 2.1 copy.97
  277.7 3.1 collective-permute-done.7
  285.8 2.6 slice_bitcast_fusion
  288.4 112.0 %while.15 = (s32[]{:T(128)}, f32[8,2,128,128]{3,2,1,0:T(8,128)}, f32[8,1152,128]{1,2,0:T(8,128)}, f32[8,1152,128]{1,2,0:T(8,128)}, bf16[8,2,128,128]{3,2,1,0:T(8...) while((s32[]{:T(128)}, f32[8,2,128,128]{3,2,1,0:T(8,128)}, ...), condition=%wide.region_6.7_spmd.clone, body=%wide.region_2.6_spmd.clone.sunk | while | flops 610160256 | bytes 15101369 | solution.py:88
  289.6 2.6 fusion.126
  299.5 2.8 fusion.131
  303.6 2.6 fusion.126
  306.2 2.1 fusion.127
  313.5 2.7 fusion.131
  317.6 2.6 fusion.126
  327.5 2.8 fusion.131
  331.6 2.6 fusion.126
  334.2 2.1 fusion.127
  341.5 2.7 fusion.131
  345.6 2.6 fusion.126
  355.5 2.8 fusion.131
  359.6 2.6 fusion.126
  369.5 2.8 fusion.131
  373.7 2.6 fusion.126
  383.5 2.8 fusion.131
  387.7 2.6 fusion.126
  397.6 2.8 fusion.131
  400.4 4.4 fusion.67
  406.8 31.4 %collective-permute-done.8 = bf16[2,128,8,128]{1,3,2,0:T(8,128)(2,1)S(1)} collective-permute-done((bf16[2,128,8,128]{1,3,2,0:T(8,128)(2,1)S(1)}, bf16[2,128,8,128]{1,3,2,0:T(8,128)(2,1)S(1)}, u32[]{:S(2)}, u32[]{:S(2)}) %collective-permute-start.8) | collective-permute-done | bytes 524320 | tf_op jit(solution)/shard_map/ppermute | solution.py:20
  440.3 20.8 %collective-permute-done.9 = bf16[2,128,8,128]{1,3,2,0:T(8,128)(2,1)S(1)} collective-permute-done((bf16[2,128,8,128]{1,3,2,0:T(8,128)(2,1)S(1)}, bf16[2,128,8,128]{1,3,2,0:T(8,128)(2,1)S(1)}, u32[]{:S(2)}, u32[]{:S(2)}) %collective-permute-start.9) | collective-permute-done | bytes 524320 | tf_op jit(solution)/shard_map/ppermute | solution.py:20
  463.1 29.6 %collective-permute-done.10 = bf16[2,128,8,128]{1,3,2,0:T(8,128)(2,1)S(1)} collective-permute-done((bf16[2,128,8,128]{1,3,2,0:T(8,128)(2,1)S(1)}, bf16[2,128,8,128]{1,3,2,0:T(8,128)(2,1)S(1)}, u32[]{:S(2)}, u32[]{:S(2)}) %collective-permute-start.10) | collective-permute-done | bytes 524320 | tf_op jit(solution)/shard_map/ppermute | solution.py:20
  495.0 20.8 %collective-permute-done.11 = bf16[2,128,8,128]{1,3,2,0:T(8,128)(2,1)S(1)} collective-permute-done((bf16[2,128,8,128]{1,3,2,0:T(8,128)(2,1)S(1)}, bf16[2,128,8,128]{1,3,2,0:T(8,128)(2,1)S(1)}, u32[]{:S(2)}, u32[]{:S(2)}) %collective-permute-start.11) | collective-permute-done | bytes 524320 | tf_op jit(solution)/shard_map/ppermute | solution.py:20
  517.9 29.4 %collective-permute-done.12 = bf16[2,128,8,128]{1,3,2,0:T(8,128)(2,1)S(1)} collective-permute-done((bf16[2,128,8,128]{1,3,2,0:T(8,128)(2,1)S(1)}, bf16[2,128,8,128]{1,3,2,0:T(8,128)(2,1)S(1)}, u32[]{:S(2)}, u32[]{:S(2)}) %collective-permute-start.12) | collective-permute-done | bytes 524320 | tf_op jit(solution)/shard_map/ppermute | solution.py:20
  549.4 21.0 %collective-permute-done.13 = bf16[2,128,8,128]{1,3,2,0:T(8,128)(2,1)S(1)} collective-permute-done((bf16[2,128,8,128]{1,3,2,0:T(8,128)(2,1)S(1)}, bf16[2,128,8,128]{1,3,2,0:T(8,128)(2,1)S(1)}, u32[]{:S(2)}, u32[]{:S(2)}) %collective-permute-start.13) | collective-permute-done | bytes 524320 | tf_op jit(solution)/shard_map/ppermute | solution.py:20
  570.6 2.2 collective-permute-start.14
  574.6 21.5 %collective-permute-done.14 = bf16[2,128,8,128]{1,3,2,0:T(8,128)(2,1)S(1)} collective-permute-done((bf16[2,128,8,128]{1,3,2,0:T(8,128)(2,1)S(1)}, bf16[2,128,8,128]{1,3,2,0:T(8,128)(2,1)S(1)}, u32[]{:S(2)}, u32[]{:S(2)}) %collective-permute-start.14) | collective-permute-done | bytes 524320 | tf_op jit(solution)/shard_map/ppermute | solution.py:20
  606.2 12.5 %collective-permute-done.15 = bf16[2,128,8,128]{1,3,2,0:T(8,128)(2,1)} collective-permute-done((bf16[2,128,8,128]{1,3,2,0:T(8,128)(2,1)}, bf16[2,128,8,128]{1,3,2,0:T(8,128)(2,1)}, u32[]{:S(2)}, u32[]{:S(2)}) %collective-permute-start.15) | collective-permute-done | bytes 524320 | tf_op jit(solution)/shard_map/ppermute | solution.py:20
  (292 shorter events, 103.1 us)
Async XLA Ops:
  0.6 224.8 %copy-start.5 = (bf16[1,128,2048]{2,1,0:T(8,128)(2,1)S(1)}, bf16[1,128,2048]{2,1,0:T(8,128)(2,1)}, u32[]{:S(2)}) copy-start(bf16[1,128,2048]{2,1,0:T(8,128)(2,1)} %param.8) | copy-start | bytes 1572868
  16.7 208.9 %copy-start.28 = (f32[128]{0:T(128)}, f32[128]{0:T(128)S(1)}, u32[]{:S(2)}) copy-start(f32[128]{0:T(128)S(1)} %get-tuple-element.183) | copy-start | bytes 1540
  16.7 236.1 %copy-start.30 = (f32[128]{0:T(128)}, f32[128]{0:T(128)S(1)}, u32[]{:S(2)}) copy-start(f32[128]{0:T(128)S(1)} %get-tuple-element.184) | copy-start | bytes 1540
  19.3 233.1 %copy-start.16 = (f32[128,64]{0,1:T(8,128)}, f32[128,64]{0,1:T(8,128)S(1)}, u32[]{:S(2)}) copy-start(f32[128,64]{0,1:T(8,128)S(1)} %get-tuple-element.185) | copy-start | bytes 98308
  19.3 233.2 %copy-start.18 = (f32[128,64]{0,1:T(8,128)}, f32[128,64]{0,1:T(8,128)S(1)}, u32[]{:S(2)}) copy-start(f32[128,64]{0,1:T(8,128)S(1)} %get-tuple-element.186) | copy-start | bytes 98308
  19.5 28.0 %collective-permute-start = (bf16[2,128,8,128]{1,3,2,0:T(8,128)(2,1)S(1)}, bf16[2,128,8,128]{1,3,2,0:T(8,128)(2,1)S(1)}, u32[]{:S(2)}, u32[]{:S(2)}) collective-permute-start(bf16[2,128,8,128]{1,3,2,0:T(8,128)(2,1)S(1)} %pad_maximum_fusion.1), channel_id=1, source_target_pairs={{0,1},{1,2},{2,3},{3,4},{4,5},{5,6},{6,7},{7,8},{8,9},{9,10},{10,1... | collective-permute-start | bytes 1572872 | tf_op jit(solution)/shard_map/ppermute | solution.py:20
  47.6 177.9 %copy-start.6 = (bf16[2,128,8,128]{1,3,2,0:T(8,128)(2,1)}, bf16[2,128,8,128]{1,3,2,0:T(8,128)(2,1)S(1)}, u32[]{:S(2)}) copy-start(bf16[2,128,8,128]{1,3,2,0:T(8,128)(2,1)S(1)} %collective-permute-done) | copy-start | bytes 1572868
  47.6 49.3 %collective-permute-start.1 = (bf16[2,128,8,128]{1,3,2,0:T(8,128)(2,1)S(1)}, bf16[2,128,8,128]{1,3,2,0:T(8,128)(2,1)S(1)}, u32[]{:S(2)}, u32[]{:S(2)}) collective-permute-start(bf16[2,128,8,128]{1,3,2,0:T(8,128)(2,1)S(1)} %collective-permute-done), channel_id=1, source_target_pairs={{0,1},{1,2},{2,3},{3,4},{4,5},{5,6},{6,7},{7,8},{8,9},{9,10},{10,1... | collective-permute-start | bytes 1572872 | tf_op jit(solution)/shard_map/ppermute | solution.py:20
  96.8 155.5 %copy-start.8 = (bf16[2,128,8,128]{1,3,2,0:T(8,128)(2,1)}, bf16[2,128,8,128]{1,3,2,0:T(8,128)(2,1)S(1)}, u32[]{:S(2)}) copy-start(bf16[2,128,8,128]{1,3,2,0:T(8,128)(2,1)S(1)} %collective-permute-done.1) | copy-start | bytes 1572868
  96.8 31.4 %collective-permute-start.2 = (bf16[2,128,8,128]{1,3,2,0:T(8,128)(2,1)S(1)}, bf16[2,128,8,128]{1,3,2,0:T(8,128)(2,1)S(1)}, u32[]{:S(2)}, u32[]{:S(2)}) collective-permute-start(bf16[2,128,8,128]{1,3,2,0:T(8,128)(2,1)S(1)} %collective-permute-done.1), channel_id=1, source_target_pairs={{0,1},{1,2},{2,3},{3,4},{4,5},{5,6},{6,7},{7,8},{8,9},{9,10},{10,1... | collective-permute-start | bytes 1572872 | tf_op jit(solution)/shard_map/ppermute | solution.py:20
  128.3 124.1 %copy-start.10 = (bf16[2,128,8,128]{1,3,2,0:T(8,128)(2,1)}, bf16[2,128,8,128]{1,3,2,0:T(8,128)(2,1)S(1)}, u32[]{:S(2)}) copy-start(bf16[2,128,8,128]{1,3,2,0:T(8,128)(2,1)S(1)} %collective-permute-done.2) | copy-start | bytes 1572868
  128.3 53.8 %collective-permute-start.3 = (bf16[2,128,8,128]{1,3,2,0:T(8,128)(2,1)S(1)}, bf16[2,128,8,128]{1,3,2,0:T(8,128)(2,1)S(1)}, u32[]{:S(2)}, u32[]{:S(2)}) collective-permute-start(bf16[2,128,8,128]{1,3,2,0:T(8,128)(2,1)S(1)} %collective-permute-done.2), channel_id=1, source_target_pairs={{0,1},{1,2},{2,3},{3,4},{4,5},{5,6},{6,7},{7,8},{8,9},{9,10},{10,1... | collective-permute-start | bytes 1572872 | tf_op jit(solution)/shard_map/ppermute | solution.py:20
  182.0 28.1 %copy-start.12 = (bf16[2,128,8,128]{1,3,2,0:T(8,128)(2,1)}, bf16[2,128,8,128]{1,3,2,0:T(8,128)(2,1)S(1)}, u32[]{:S(2)}) copy-start(bf16[2,128,8,128]{1,3,2,0:T(8,128)(2,1)S(1)} %collective-permute-done.3) | copy-start | bytes 1572868
  182.0 28.1 %collective-permute-start.4 = (bf16[2,128,8,128]{1,3,2,0:T(8,128)(2,1)S(1)}, bf16[2,128,8,128]{1,3,2,0:T(8,128)(2,1)S(1)}, u32[]{:S(2)}, u32[]{:S(2)}) collective-permute-start(bf16[2,128,8,128]{1,3,2,0:T(8,128)(2,1)S(1)} %collective-permute-done.3), channel_id=1, source_target_pairs={{0,1},{1,2},{2,3},{3,4},{4,5},{5,6},{6,7},{7,8},{8,9},{9,10},{10,1... | collective-permute-start | bytes 1572872 | tf_op jit(solution)/shard_map/ppermute | solution.py:20
  210.2 41.8 %copy-start.14 = (bf16[2,128,8,128]{1,3,2,0:T(8,128)(2,1)}, bf16[2,128,8,128]{1,3,2,0:T(8,128)(2,1)S(1)}, u32[]{:S(2)}) copy-start(bf16[2,128,8,128]{1,3,2,0:T(8,128)(2,1)S(1)} %collective-permute-done.4) | copy-start | bytes 1572868
  210.2 26.4 %collective-permute-start.5 = (bf16[2,128,8,128]{1,3,2,0:T(8,128)(2,1)S(1)}, bf16[2,128,8,128]{1,3,2,0:T(8,128)(2,1)}, u32[]{:S(2)}, u32[]{:S(2)}) collective-permute-start(bf16[2,128,8,128]{1,3,2,0:T(8,128)(2,1)S(1)} %collective-permute-done.4), channel_id=1, source_target_pairs={{0,1},{1,2},{2,3},{3,4},{4,5},{5,6},{6,7},{7,8},{8,9},{9,10},{10,1... | collective-permute-start | bytes 1572872 | tf_op jit(solution)/shard_map/ppermute | solution.py:20
  236.6 22.6 %collective-permute-start.6 = (bf16[2,128,8,128]{1,3,2,0:T(8,128)(2,1)}, bf16[2,128,8,128]{1,3,2,0:T(8,128)(2,1)}, u32[]{:S(2)}, u32[]{:S(2)}) collective-permute-start(bf16[2,128,8,128]{1,3,2,0:T(8,128)(2,1)} %collective-permute-done.5), channel_id=1, source_target_pairs={{0,1},{1,2},{2,3},{3,4},{4,5},{5,6},{6,7},{7,8},{8,9},{9,10},{10,1... | collective-permute-start | bytes 1572872 | tf_op jit(solution)/shard_map/ppermute | solution.py:20
  252.6 22.4 %copy-start.3 = (f32[128,64]{1,0:T(8,128)}, f32[128,64]{1,0:T(8,128)S(1)}, u32[]{:S(2)}) copy-start(f32[128,64]{1,0:T(8,128)S(1)} %copy.92) | copy-start | bytes 98308
  252.6 22.3 %copy-start.20 = (f32[128,16]{0,1:T(8,128)}, f32[128,16]{0,1:T(8,128)S(1)}, u32[]{:S(2)}) copy-start(f32[128,16]{0,1:T(8,128)S(1)} %copy.88) | copy-start | bytes 24580
  259.2 21.6 %collective-permute-start.7 = (bf16[2,128,8,128]{1,3,2,0:T(8,128)(2,1)}, bf16[2,128,8,128]{1,3,2,0:T(8,128)(2,1)}, u32[]{:S(2)}, u32[]{:S(2)}) collective-permute-start(bf16[2,128,8,128]{1,3,2,0:T(8,128)(2,1)} %collective-permute-done.6), channel_id=1, source_target_pairs={{0,1},{1,2},{2,3},{3,4},{4,5},{5,6},{6,7},{7,8},{8,9},{9,10},{10,1... | collective-permute-start | bytes 1572872 | tf_op jit(solution)/shard_map/ppermute | solution.py:20
  277.4 7.1 %copy-start.15 = (bf16[2,128,8,128]{1,3,2,0:T(8,128)(2,1)S(1)}, bf16[2,128,8,128]{1,3,2,0:T(8,128)(2,1)}, u32[]{:S(2)}) copy-start(bf16[2,128,8,128]{1,3,2,0:T(8,128)(2,1)} %copy-done.14) | copy-start | bytes 1572868
  277.7 6.9 %copy-start.13 = (bf16[2,128,8,128]{1,3,2,0:T(8,128)(2,1)S(1)}, bf16[2,128,8,128]{1,3,2,0:T(8,128)(2,1)}, u32[]{:S(2)}) copy-start(bf16[2,128,8,128]{1,3,2,0:T(8,128)(2,1)} %copy-done.12) | copy-start | bytes 1572868
  288.4 7.7 %copy-start.1 = (bf16[8,2,128,128]{3,2,1,0:T(8,128)(2,1)}, bf16[8,2,128,128]{3,2,1,0:T(8,128)(2,1)S(1)}, u32[]{:S(2)}) copy-start(bf16[8,2,128,128]{3,2,1,0:T(8,128)(2,1)S(1)} %get-tuple-element.296) | copy-start | bytes 1572868 | tf_op jit(solution)/shard_map/while
  302.3 6.0 copy-start.24
  302.3 6.0 copy-start.26
  302.3 7.8 %copy-start.1 = (bf16[8,2,128,128]{3,2,1,0:T(8,128)(2,1)}, bf16[8,2,128,128]{3,2,1,0:T(8,128)(2,1)S(1)}, u32[]{:S(2)}) copy-start(bf16[8,2,128,128]{3,2,1,0:T(8,128)(2,1)S(1)} %get-tuple-element.296) | copy-start | bytes 1572868 | tf_op jit(solution)/shard_map/while
  316.3 6.0 copy-start.24
  316.3 7.8 %copy-start.1 = (bf16[8,2,128,128]{3,2,1,0:T(8,128)(2,1)}, bf16[8,2,128,128]{3,2,1,0:T(8,128)(2,1)S(1)}, u32[]{:S(2)}) copy-start(bf16[8,2,128,128]{3,2,1,0:T(8,128)(2,1)S(1)} %get-tuple-element.296) | copy-start | bytes 1572868 | tf_op jit(solution)/shard_map/while
  330.3 6.0 copy-start.24
  330.3 6.0 copy-start.26
  330.3 7.8 %copy-start.1 = (bf16[8,2,128,128]{3,2,1,0:T(8,128)(2,1)}, bf16[8,2,128,128]{3,2,1,0:T(8,128)(2,1)S(1)}, u32[]{:S(2)}) copy-start(bf16[8,2,128,128]{3,2,1,0:T(8,128)(2,1)S(1)} %get-tuple-element.296) | copy-start | bytes 1572868 | tf_op jit(solution)/shard_map/while
  344.3 7.8 %copy-start.1 = (bf16[8,2,128,128]{3,2,1,0:T(8,128)(2,1)}, bf16[8,2,128,128]{3,2,1,0:T(8,128)(2,1)S(1)}, u32[]{:S(2)}) copy-start(bf16[8,2,128,128]{3,2,1,0:T(8,128)(2,1)S(1)} %get-tuple-element.296) | copy-start | bytes 1572868 | tf_op jit(solution)/shard_map/while
  358.3 7.8 %copy-start.1 = (bf16[8,2,128,128]{3,2,1,0:T(8,128)(2,1)}, bf16[8,2,128,128]{3,2,1,0:T(8,128)(2,1)S(1)}, u32[]{:S(2)}) copy-start(bf16[8,2,128,128]{3,2,1,0:T(8,128)(2,1)S(1)} %get-tuple-element.296) | copy-start | bytes 1572868 | tf_op jit(solution)/shard_map/while
  372.4 7.8 %copy-start.1 = (bf16[8,2,128,128]{3,2,1,0:T(8,128)(2,1)}, bf16[8,2,128,128]{3,2,1,0:T(8,128)(2,1)S(1)}, u32[]{:S(2)}) copy-start(bf16[8,2,128,128]{3,2,1,0:T(8,128)(2,1)S(1)} %get-tuple-element.296) | copy-start | bytes 1572868 | tf_op jit(solution)/shard_map/while
  386.4 7.8 %copy-start.1 = (bf16[8,2,128,128]{3,2,1,0:T(8,128)(2,1)}, bf16[8,2,128,128]{3,2,1,0:T(8,128)(2,1)S(1)}, u32[]{:S(2)}) copy-start(bf16[8,2,128,128]{3,2,1,0:T(8,128)(2,1)S(1)} %get-tuple-element.296) | copy-start | bytes 1572868 | tf_op jit(solution)/shard_map/while
  404.9 33.3 %collective-permute-start.8 = (bf16[2,128,8,128]{1,3,2,0:T(8,128)(2,1)S(1)}, bf16[2,128,8,128]{1,3,2,0:T(8,128)(2,1)S(1)}, u32[]{:S(2)}, u32[]{:S(2)}) collective-permute-start(bf16[2,128,8,128]{1,3,2,0:T(8,128)(2,1)S(1)} %slice.95), channel_id=1, source_target_pairs={{1,0},{2,1},{3,2},{4,3},{5,4},{6,5},{7,6},{8,7},{9,8},{10,9},{11,1... | collective-permute-start | bytes 1572872 | tf_op jit(solution)/shard_map/ppermute | solution.py:20
  438.3 22.7 %collective-permute-start.9 = (bf16[2,128,8,128]{1,3,2,0:T(8,128)(2,1)S(1)}, bf16[2,128,8,128]{1,3,2,0:T(8,128)(2,1)S(1)}, u32[]{:S(2)}, u32[]{:S(2)}) collective-permute-start(bf16[2,128,8,128]{1,3,2,0:T(8,128)(2,1)S(1)} %add_convert_fusion.6), channel_id=1, source_target_pairs={{1,0},{2,1},{3,2},{4,3},{5,4},{6,5},{7,6},{8,7},{9,8},{10,9},{11,1... | collective-permute-start | bytes 1572872 | tf_op jit(solution)/shard_map/ppermute | solution.py:20
  461.2 31.5 %collective-permute-start.10 = (bf16[2,128,8,128]{1,3,2,0:T(8,128)(2,1)S(1)}, bf16[2,128,8,128]{1,3,2,0:T(8,128)(2,1)S(1)}, u32[]{:S(2)}, u32[]{:S(2)}) collective-permute-start(bf16[2,128,8,128]{1,3,2,0:T(8,128)(2,1)S(1)} %add_convert_fusion.5), channel_id=1, source_target_pairs={{1,0},{2,1},{3,2},{4,3},{5,4},{6,5},{7,6},{8,7},{9,8},{10,9},{11,1... | collective-permute-start | bytes 1572872 | tf_op jit(solution)/shard_map/ppermute | solution.py:20
  492.9 79.9 %copy-start = (f32[8,2,128,128]{3,2,1,0:T(8,128)S(1)}, f32[8,2,128,128]{3,2,1,0:T(8,128)}, u32[]{:S(2)}) copy-start(f32[8,2,128,128]{3,2,1,0:T(8,128)} %get-tuple-element.52) | copy-start | bytes 3145732
  493.0 22.8 %collective-permute-start.11 = (bf16[2,128,8,128]{1,3,2,0:T(8,128)(2,1)S(1)}, bf16[2,128,8,128]{1,3,2,0:T(8,128)(2,1)S(1)}, u32[]{:S(2)}, u32[]{:S(2)}) collective-permute-start(bf16[2,128,8,128]{1,3,2,0:T(8,128)(2,1)S(1)} %add_convert_fusion.4), channel_id=1, source_target_pairs={{1,0},{2,1},{3,2},{4,3},{5,4},{6,5},{7,6},{8,7},{9,8},{10,9},{11,1... | collective-permute-start | bytes 1572872 | tf_op jit(solution)/shard_map/ppermute | solution.py:20
  516.0 31.3 %collective-permute-start.12 = (bf16[2,128,8,128]{1,3,2,0:T(8,128)(2,1)S(1)}, bf16[2,128,8,128]{1,3,2,0:T(8,128)(2,1)S(1)}, u32[]{:S(2)}, u32[]{:S(2)}) collective-permute-start(bf16[2,128,8,128]{1,3,2,0:T(8,128)(2,1)S(1)} %add_convert_fusion.3), channel_id=1, source_target_pairs={{1,0},{2,1},{3,2},{4,3},{5,4},{6,5},{7,6},{8,7},{9,8},{10,9},{11,1... | collective-permute-start | bytes 1572872 | tf_op jit(solution)/shard_map/ppermute | solution.py:20
  547.5 23.0 %collective-permute-start.13 = (bf16[2,128,8,128]{1,3,2,0:T(8,128)(2,1)S(1)}, bf16[2,128,8,128]{1,3,2,0:T(8,128)(2,1)S(1)}, u32[]{:S(2)}, u32[]{:S(2)}) collective-permute-start(bf16[2,128,8,128]{1,3,2,0:T(8,128)(2,1)S(1)} %add_convert_fusion.2), channel_id=1, source_target_pairs={{1,0},{2,1},{3,2},{4,3},{5,4},{6,5},{7,6},{8,7},{9,8},{10,9},{11,1... | collective-permute-start | bytes 1572872 | tf_op jit(solution)/shard_map/ppermute | solution.py:20
  570.6 25.4 %collective-permute-start.14 = (bf16[2,128,8,128]{1,3,2,0:T(8,128)(2,1)S(1)}, bf16[2,128,8,128]{1,3,2,0:T(8,128)(2,1)S(1)}, u32[]{:S(2)}, u32[]{:S(2)}) collective-permute-start(bf16[2,128,8,128]{1,3,2,0:T(8,128)(2,1)S(1)} %add_convert_fusion.1), channel_id=1, source_target_pairs={{1,0},{2,1},{3,2},{4,3},{5,4},{6,5},{7,6},{8,7},{9,8},{10,9},{11,1... | collective-permute-start | bytes 1572872 | tf_op jit(solution)/shard_map/ppermute | solution.py:20
  573.3 25.7 %copy-start.31 = (f32[128]{0:T(128)S(1)}, f32[128]{0:T(128)}, u32[]{:S(2)}) copy-start(f32[128]{0:T(128)} %copy-done.30) | copy-start | bytes 1540
  574.6 25.7 %copy-start.21 = (f32[128,16]{0,1:T(8,128)S(1)}, f32[128,16]{0,1:T(8,128)}, u32[]{:S(2)}) copy-start(f32[128,16]{0,1:T(8,128)} %copy-done.20) | copy-start | bytes 24580
  597.0 21.6 %collective-permute-start.15 = (bf16[2,128,8,128]{1,3,2,0:T(8,128)(2,1)}, bf16[2,128,8,128]{1,3,2,0:T(8,128)(2,1)}, u32[]{:S(2)}, u32[]{:S(2)}) collective-permute-start(bf16[2,128,8,128]{1,3,2,0:T(8,128)(2,1)} %add_convert_fusion), channel_id=1, source_target_pairs={{1,0},{2,1},{3,2},{4,3},{5,4},{6,5},{7,6},{8,7},{9,8},{10,9},{11,1... | collective-permute-start | bytes 1572872 | tf_op jit(solution)/shard_map/ppermute | solution.py:20
  606.2 14.1 %copy-start.17 = (f32[128,64]{0,1:T(8,128)S(1)}, f32[128,64]{0,1:T(8,128)}, u32[]{:S(2)}) copy-start(f32[128,64]{0,1:T(8,128)} %copy-done.16) | copy-start | bytes 98308
  606.2 14.1 %copy-start.19 = (f32[128,64]{0,1:T(8,128)S(1)}, f32[128,64]{0,1:T(8,128)}, u32[]{:S(2)}) copy-start(f32[128,64]{0,1:T(8,128)} %copy-done.18) | copy-start | bytes 98308
  (42 other events, 144.4 us)
where the time goes:
time: 625 us; the launch traced here: 622 us
  waiting for transfers between devices  292 us (47%)
  starting transfers between devices  167 us (27%)
  matrix products  92.1 us (15%)
  local copies, waits for them, and re-layouts  35.6 us (6%)
  other arithmetic  18.1 us (3%)
  blocking collectives  15.2 us (2%)
    ppermute x16, waiting for transfers between devices, passed_along(): return lax.ppermute(block, axis, route)  292 us
    ppermute x16, starting transfers between devices, passed_along(): return lax.ppermute(block, axis, route)  167 us
    dot_general x8, matrix products, attend_head(): jnp.einsum('gtl,gtd->ld', probs_b, grad_group, preferred_element_type=jnp...  22.1 us
    sub x8, matrix products, attend_head(): weights = jnp.exp(scores - row_max)  20.9 us
    dot_general x8, matrix products, attend_head(): jnp.einsum('gtl,ld->gtd', probs_b, value_block, preferred_element_type=jn...  16.5 us
    dot_general x8, matrix products, attend_head(): jnp.einsum('gtl,ld->gtd', dscore_b, key_block, preferred_element_type=jnp...  15.5 us
    all_gather x1, blocking collectives, body(): lax.all_gather(jnp.stack([query_gain, key_norm_gain]), 'dp', axis=1, tile...  15.2 us
    dot_general x8, matrix products, attend_head(): jnp.einsum('gtd,ld->gtl', grad_group, value_block, preferred_element_type...  14.2 us
  transfers between devices with their start and end apart: 16, of which 16 were waited for; matrix products, arithmetic and copies ran while one was open for 2% of the time, Pallas kernels for 0%

commit v1 on v0

v1 whole, which is shorter than its diff:
```python
import functools

import jax
import jax.numpy as jnp
import numpy as np
from jax import lax
from jax.experimental import pallas as pl
from jax.experimental.pallas import tpu as pltpu
from jax.sharding import PartitionSpec as P

HEAD = 128
GROUP = 8
TOK = 128
SPAN = GROUP * TOK
WINDOW = 1024
SCALE = 168.0 ** (-0.5)
LOG2E = 1.4426950408889634
ROPE_BASE = 10000.0
EPSILON = 1e-06
NT = (((1,), (1,)), ((), ()))
NN = (((1,), (0,)), ((), ()))


def mm(a, b, dims):
    return lax.dot_general(a, b, dims, preferred_element_type=jnp.float32)


def inverse_norm(x):
    return lax.rsqrt(jnp.mean(x * x, axis=-1, keepdims=True) + EPSILON)


def rotate(n, cosine, sine):
    return n * cosine + pltpu.roll(n, HEAD // 2, 1) * sine


def prepare(x, gain, cosine, sine):
    return rotate(x * inverse_norm(x) * gain, cosine, sine)


def prepare_back(x, gain, cosine, sine, dy):
    inv = inverse_norm(x)
    h = (dy * cosine + pltpu.roll(dy * sine, HEAD // 2, 1)) * gain
    return inv * h - x * (inv * inv * inv * jnp.mean(x * h, axis=-1, keepdims=True))


def attend_kernel(
    low_ref, qd_ref, kv_ref, prev_ref, gain_ref, cos_ref, sin_ref,
    qg_ref, remote_ref, own_ref,
    k_s, kt_s, v_s, dk_s, dv_s,
):
    low = low_ref[0]
    q_gain = gain_ref[0:1, :]
    k_gain = gain_ref[1:2, :]

    def load_keys(i, _):
        for base, src in ((0, prev_ref), (SPAN, kv_ref)):
            rows = pl.ds(pl.multiple_of(i * TOK, TOK), TOK)
            at = pl.ds(pl.multiple_of(base + i * TOK, TOK), TOK)
            block = src[rows, :]
            hat = prepare(block[:, :HEAD].astype(jnp.float32), k_gain, cos_ref[at, :], sin_ref[at, :])
            k_s[at, :] = hat.astype(jnp.bfloat16)
            kt_s[:, at] = hat.T.astype(jnp.bfloat16)
            v_s[at, :] = block[:, HEAD:]
            dk_s[at, :] = jnp.zeros((TOK, HEAD), jnp.float32)
            dv_s[at, :] = jnp.zeros((TOK, HEAD), jnp.float32)
        return 0

    lax.fori_loop(0, GROUP, load_keys, 0)

    wide = WINDOW + TOK

    def step(b, _):
        rows = pl.ds(pl.multiple_of(b * TOK, TOK), TOK)
        at = pl.ds(pl.multiple_of(SPAN + b * TOK, TOK), TOK)
        keys = pl.ds(pl.multiple_of(b * TOK, TOK), wide)
        cosine, sine = cos_ref[at, :], sin_ref[at, :]
        raw = [qd_ref[rows, h * HEAD : (h + 1) * HEAD].astype(jnp.float32) for h in range(2)]
        q = jnp.concatenate([prepare(x, q_gain, cosine, sine) for x in raw], axis=0).astype(jnp.bfloat16)
        do = jnp.concatenate(
            [qd_ref[rows, (2 + h) * HEAD : (3 + h) * HEAD] for h in range(2)], axis=0
        )
        s = mm(k_s[keys, :], q, NT)
        row = lax.broadcasted_iota(jnp.int32, (wide, 2 * TOK), 0)
        col = lax.broadcasted_iota(jnp.int32, (wide, 2 * TOK), 1) % TOK
        seen = (row > col) & (row <= col + WINDOW) & (row >= low - b * TOK)
        s = jnp.where(seen, s * (SCALE * LOG2E), -1e30)
        w = jnp.exp2(s - jnp.max(s, axis=0, keepdims=True))
        probs = w * (1.0 / jnp.sum(w, axis=0, keepdims=True))
        pb = probs.astype(jnp.bfloat16)
        dp = mm(v_s[keys, :], do, NT)
        delta = jnp.sum(pb.astype(jnp.float32) * dp, axis=0, keepdims=True)
        ds = (probs * (dp - delta)).astype(jnp.bfloat16)
        dv_s[keys, :] += mm(pb, do, NN)
        dk_s[keys, :] += mm(ds, q, NN)
        dq = (mm(kt_s[:, keys], ds, NN) * SCALE).T
        for h in range(2):
            back = prepare_back(raw[h], q_gain, cosine, sine, dq[h * TOK : (h + 1) * TOK, :])
            qg_ref[rows, h * HEAD : (h + 1) * HEAD] = back.astype(jnp.bfloat16)
        return 0

    lax.fori_loop(0, GROUP, step, 0)

    remote_ref[:, :HEAD] = (dk_s[:SPAN, :] * SCALE).astype(jnp.bfloat16)
    remote_ref[:, HEAD:] = dv_s[:SPAN, :].astype(jnp.bfloat16)
    own_ref[:, :HEAD] = dk_s[SPAN:, :] * SCALE
    own_ref[:, HEAD:] = dv_s[SPAN:, :]


def finish_kernel(own_ref, back_ref, kv_ref, gain_ref, cos_ref, sin_ref, out_ref):
    total = own_ref[...] + back_ref[...].astype(jnp.float32)
    raw = kv_ref[:, :HEAD].astype(jnp.float32)
    dk = prepare_back(raw, gain_ref[1:2, :], cos_ref[...], sin_ref[...], total[:, :HEAD])
    out_ref[:, :HEAD] = dk.astype(jnp.bfloat16)
    out_ref[:, HEAD:] = total[:, HEAD:].astype(jnp.bfloat16)


VM = pl.BlockSpec(memory_space=pltpu.VMEM)
SM = pl.BlockSpec(memory_space=pltpu.SMEM)


def routes(mesh):
    n_seq = mesh.shape["seq"]
    groups = n_seq // GROUP

    def device(x, z, low):
        return (z % 8) * n_seq + (x * 2 + z // 8) * GROUP + low

    plan = {}
    for sign in (1, -1):
        first, second = [], []
        for x in range(groups // 2):
            for z in range(16):
                if x * 2 + z // 8 + 1 == groups:
                    continue
                mid = (z + 4 * sign) % 16
                end = (z + 8) % 16
                for low in range(GROUP):
                    first.append((device(x, z, low), device(x, mid, low)))
                    second.append((device(x, mid, low), device(x + z // 8, end, low)))
        plan[sign] = (first, second)
    return plan


def carry(block, plan, back):
    half = block.shape[0] // 2
    parts = []
    for sign, part in ((1, block[:half]), (-1, block[half:])):
        legs = plan[sign]
        if back:
            legs = [[(b, a) for a, b in leg] for leg in legs[::-1]]
        for leg in legs:
            part = lax.ppermute(part, ("dp", "seq"), leg)
        parts.append(part)
    return jnp.concatenate(parts, axis=0)


def body(plan, n_seq, queries, raw_key_rows, values, out_grad, query_gain, key_norm_gain):
    members = [[g * GROUP + i for i in range(GROUP)] for g in range(n_seq // GROUP)]
    swap = functools.partial(
        lax.all_to_all, axis_name="seq", split_axis=0, concat_axis=0, axis_index_groups=members
    )

    def by_head(x):
        return x[0].reshape(TOK, GROUP, -1).transpose(1, 0, 2)

    kv = swap(jnp.concatenate([by_head(raw_key_rows), by_head(values)], axis=-1))
    kv = kv.reshape(SPAN, 2 * HEAD)
    prev = carry(kv, plan, False)
    qd = swap(jnp.concatenate([by_head(queries), by_head(out_grad)], axis=-1))
    qd = qd.reshape(SPAN, 4 * HEAD)

    dp = lax.axis_index("dp")
    n_dp = lax.axis_size("dp")
    part = jnp.stack([query_gain, key_norm_gain])
    gains = lax.dynamic_update_slice(jnp.zeros((2, HEAD), jnp.float32), part, (0, dp * part.shape[1]))
    for bit in (1, 2, 4):
        gains = gains + lax.ppermute(gains, "dp", [(i, i ^ bit) for i in range(n_dp)])

    group = lax.axis_index("seq") // GROUP
    positions = (group - 1) * SPAN + jnp.arange(2 * SPAN, dtype=jnp.int32)
    frequency = ROPE_BASE ** (-jnp.arange(HEAD // 2).astype(jnp.float32) * (2.0 / HEAD))
    angles = positions.astype(jnp.float32)[:, None] * frequency[None, :]
    cosine, sine = jnp.cos(angles), jnp.sin(angles)
    cosine = jnp.concatenate([cosine, cosine], axis=-1)
    sine = jnp.concatenate([-sine, sine], axis=-1)
    low = jnp.where(group == 0, SPAN, 0).astype(jnp.int32).reshape(1)

    qg, remote, own = pl.pallas_call(
        attend_kernel,
        out_shape=(
            jax.ShapeDtypeStruct((SPAN, 2 * HEAD), jnp.bfloat16),
            jax.ShapeDtypeStruct((SPAN, 2 * HEAD), jnp.bfloat16),
            jax.ShapeDtypeStruct((SPAN, 2 * HEAD), jnp.float32),
        ),
        in_specs=[SM] + [VM] * 6,
        out_specs=(VM, VM, VM),
        scratch_shapes=[
            pltpu.VMEM((2 * SPAN, HEAD), jnp.bfloat16),
            pltpu.VMEM((HEAD, 2 * SPAN), jnp.bfloat16),
            pltpu.VMEM((2 * SPAN, HEAD), jnp.bfloat16),
            pltpu.VMEM((2 * SPAN, HEAD), jnp.float32),
            pltpu.VMEM((2 * SPAN, HEAD), jnp.float32),
        ],
        cost_estimate=pl.CostEstimate(flops=4 * 10**9, bytes_accessed=8 * 2**20, transcendentals=2 * 10**6),
        name="attend",
    )(low, qd, kv, prev, gains, cosine, sine)

    back = carry(remote, plan, True)
    qg = swap(qg.reshape(GROUP, TOK, 2 * HEAD))
    kvg = pl.pallas_call(
        finish_kernel,
        out_shape=jax.ShapeDtypeStruct((SPAN, 2 * HEAD), jnp.bfloat16),
        in_specs=[VM] * 6,
        out_specs=VM,
        name="finish",
    )(own, back, kv, gains, cosine[SPAN:], sine[SPAN:])
    kvg = swap(kvg.reshape(GROUP, TOK, 2 * HEAD))

    def by_token(x):
        return x.transpose(1, 0, 2).reshape(1, TOK, -1)

    return by_token(qg), by_token(kvg[:, :, :HEAD]), by_token(kvg[:, :, HEAD:])


def solution(mesh):
    spec = P("dp", "seq", None)
    return jax.shard_map(
        functools.partial(body, routes(mesh), mesh.shape["seq"]),
        mesh=mesh,
        in_specs=(spec, spec, spec, spec, P("dp"), P("dp")),
        out_specs=(spec, spec, spec),
        check_vma=False,
    )
```

time: 625 us -> 202 us (0.32)
  the two profiles are of different devices: /device:TPU:125 before, /device:TPU:4 now
where the time goes in v1:
time: 202 us
  starting transfers between devices  84.6 us (42%)
  waiting for transfers between devices  71 us (35%)
  Pallas kernels  23.1 us (11%)
  other arithmetic  12.9 us (6%)
  local copies, waits for them, and re-layouts  9.01 us (4%)
    ppermute x8, waiting for transfers between devices, carry(): part = lax.ppermute(part, ('dp', 'seq'), leg)  59.7 us
    ppermute x8, starting transfers between devices, carry(): part = lax.ppermute(part, ('dp', 'seq'), leg)  48.5 us
    pallas_call x1, Pallas kernels, body(): pl.pallas_call(attend_kernel, out_shape=(jax.ShapeDtypeStruct((SPAN, 2 *...  20 us
    ppermute x3, starting transfers between devices, body(): lax.ppermute(gains, 'dp', [(i, i ^ bit) for i in range(n_dp)])  14.6 us
    all_to_all x1, starting transfers between devices, body(): kvg = swap(kvg.reshape(GROUP, TOK, 2 * HEAD))  8.29 us
    all_to_all x1, waiting for transfers between devices, body(): kvg = swap(kvg.reshape(GROUP, TOK, 2 * HEAD))  7.98 us
    all_to_all x1, starting transfers between devices, body(): swap(jnp.concatenate([by_head(raw_key_rows), by_head(values)], axis=-1))  4.6 us
    all_to_all x1, starting transfers between devices, body(): qg = swap(qg.reshape(GROUP, TOK, 2 * HEAD))  4.32 us
  transfers between devices with their start and end apart: 15, of which 7 were waited for; matrix products, arithmetic and copies ran while one was open for 9% of the time, Pallas kernels for 2%

profile of v1, /device:TPU:4, one launch (start us, length us, event | category | flops | bytes accessed | tf_op | source)
XLA Modules:
  0.0 201.6 jit_solution(3582611557756605941)
XLA Ops:
  0.6 0.7 pad_maximum_fusion.6
  1.3 0.1 dynamic_update_slice.5
  1.5 3.9 %collective-permute-start.4 = (f32[2,128]{1,0:T(2,128)S(1)}, f32[2,128]{1,0:T(2,128)S(1)}, u32[]{:S(2)}, u32[]{:S(2)}) collective-permute-start(f32[2,128]{1,0:T(2,128)S(1)} %dynamic_update_slice.5), channel_id=1, source_target_pairs={{0,64},{64,0},{128,192},{192,128},{256,320},{320,256},{384,448},{4... | collective-permute-start | bytes 3080 | tf_op jit(solution)/shard_map/ppermute | solution.py:177
  5.4 1.0 copy.18
  6.4 1.0 copy.19
  7.4 0.1 copy_bitcast_fusion.2
  7.5 0.9 pad_maximum_fusion.3
  8.4 4.6 %all-to-all-start.1 = ((bf16[8,128,256]{2,1,0:T(8,128)(2,1)}), bf16[8,128,256]{2,1,0:T(8,128)(2,1)S(1)}, u32[]{:S(2)}, u32[]{:S(2)}) async-start(bf16[8,128,256]{2,1,0:T(8,128)(2,1)} %pad_maximum_fusion.3), calls=%async_computation.1 | async-start | bytes 1048576 | tf_op jit(solution)/shard_map/all_to_all | solution.py:166
  13.0 0.1 copy.16
  13.1 0.1 copy.17
  13.2 0.2 copy_bitcast_fusion
  13.5 1.1 pad_maximum_fusion
  14.8 5.3 %collective-permute-start.5 = (f32[2,128]{1,0:T(2,128)S(1)}, f32[2,128]{1,0:T(2,128)S(1)}, u32[]{:S(2)}, u32[]{:S(2)}) collective-permute-start(f32[2,128]{1,0:T(2,128)S(1)} %add.26), channel_id=1, source_target_pairs={{0,128},{64,192},{128,0},{192,64},{256,384},{320,448},{384,256},{4... | collective-permute-start | bytes 3080 | tf_op jit(solution)/shard_map/ppermute | solution.py:177
  20.0 3.3 %all-to-all-done.1 = bf16[8,128,256]{2,1,0:T(8,128)(2,1)S(1)} async-done(((bf16[8,128,256]{2,1,0:T(8,128)(2,1)}), bf16[8,128,256]{2,1,0:T(8,128)(2,1)S(1)}, u32[]{:S(2)}, u32[]{:S(2)}) %all-to-all-start.1) | async-done | bytes 524320 | tf_op jit(solution)/shard_map/all_to_all | solution.py:166
  23.3 4.2 %all-to-all-start = ((bf16[8,128,512]{2,1,0:T(8,128)(2,1)}), bf16[8,128,512]{2,1,0:T(8,128)(2,1)}, u32[]{:S(2)}, u32[]{:S(2)}) async-start(bf16[8,128,512]{2,1,0:T(8,128)(2,1)} %pad_maximum_fusion), calls=%async_computation | async-start | bytes 2097152 | tf_op jit(solution)/shard_map/all_to_all | solution.py:169
  27.6 11.9 %collective-permute-start.2 = (bf16[512,256]{1,0:T(8,128)(2,1)S(1)}, bf16[512,256]{1,0:T(8,128)(2,1)}, u32[]{:S(2)}, u32[]{:S(2)}) collective-permute-start(bf16[512,256]{1,0:T(8,128)(2,1)S(1)} %bitcast.47), channel_id=1, source_target_pairs={{0,264},{1,265},{2,266},{3,267},{4,268},{5,269},{6,270},{7,271},{6... | collective-permute-start | bytes 786440 | tf_op jit(solution)/shard_map/ppermute | solution.py:152
  39.5 1.9 collective-permute-start
  41.4 3.7 %fusion.2 = (f32[2048,64]{1,0:T(8,128)S(1)}, f32[2048,64]{1,0:T(8,128)S(1)}, f32[2048,64]{1,0:T(8,128)S(1)}) fusion(f32[64]{0:T(128)S(1)} %multiply_power_fusion, f32[2048]{0:T(1024)S(1)} %add_convert_fusion), kind=kLoop, calls=%fused_computation.16 | loop fusion | flops 262144 | bytes 1581312 | tf_op jit(solution)/shard_map/neg | solution.py:185
  45.2 5.5 %collective-permute-start.6 = (f32[2,128]{1,0:T(2,128)S(1)}, f32[2,128]{1,0:T(2,128)S(1)}, u32[]{:S(2)}, u32[]{:S(2)}) collective-permute-start(f32[2,128]{1,0:T(2,128)S(1)} %add.27), channel_id=1, source_target_pairs={{0,256},{64,320},{128,384},{192,448},{256,0},{320,64},{384,128},{4... | collective-permute-start | bytes 3080 | tf_op jit(solution)/shard_map/ppermute | solution.py:177
  50.6 9.6 %collective-permute-done.2 = bf16[512,256]{1,0:T(8,128)(2,1)} collective-permute-done((bf16[512,256]{1,0:T(8,128)(2,1)S(1)}, bf16[512,256]{1,0:T(8,128)(2,1)}, u32[]{:S(2)}, u32[]{:S(2)}) %collective-permute-start.2) | collective-permute-done | bytes 262176 | tf_op jit(solution)/shard_map/ppermute | solution.py:152
  60.3 7.1 %collective-permute-start.3 = (bf16[512,256]{1,0:T(8,128)(2,1)}, bf16[512,256]{1,0:T(8,128)(2,1)S(1)}, u32[]{:S(2)}, u32[]{:S(2)}) collective-permute-start(bf16[512,256]{1,0:T(8,128)(2,1)} %collective-permute-done.2), channel_id=1, source_target_pairs={{264,8},{265,9},{266,10},{267,11},{268,12},{269,13},{270,14},{271,... | collective-permute-start | bytes 786440 | tf_op jit(solution)/shard_map/ppermute | solution.py:152
  67.4 1.9 collective-permute-start.1
  69.3 1.9 pad_maximum_fusion.1
  71.2 0.6 add.28.gain_ref
  71.8 20.1 %collective-permute-done.3 = bf16[512,256]{1,0:T(8,128)(2,1)S(1)} collective-permute-done((bf16[512,256]{1,0:T(8,128)(2,1)}, bf16[512,256]{1,0:T(8,128)(2,1)S(1)}, u32[]{:S(2)}, u32[]{:S(2)}) %collective-permute-start.3) | collective-permute-done | bytes 262176 | tf_op jit(solution)/shard_map/ppermute | solution.py:152
  91.9 1.8 pad_maximum_fusion.4.prev_ref
  93.7 20.0 %attend.1 = (bf16[1024,256]{1,0:T(8,128)(2,1)}, bf16[1024,256]{1,0:T(8,128)(2,1)}, f32[1024,256]{1,0:T(8,128)}) custom-call(s32[1]{0:T(128)} %bitcast.low_ref, bf16[1024,512]{1,0:T(8,128)(2,1)} %bitcast.3.qd_ref, bf16[1024,256]{1,0:T(8,128)(2,1)} %bitcast.34, bf16[1024,256]{1,0:T(8,128)(2,1)} %pad_maximum_fusion.4.prev_ref, f32[2,128]{1,0:T(2,128)} %add.28.gain_ref, ...), custom_call_target="tpu_custom_call" | custom-call | flops 4000000000 | bytes 8388608 | tf_op jit(solution)/shard_map/attend/pallas_call | solution.py:188
  113.6 1.8 fusion.3
  115.4 11.5 %collective-permute-start.7 = (bf16[512,256]{1,0:T(8,128)(2,1)}, bf16[512,256]{1,0:T(8,128)(2,1)}, u32[]{:S(2)}, u32[]{:S(2)}) collective-permute-start(bf16[512,256]{1,0:T(8,128)(2,1)} %get-tuple-element.11), channel_id=1, source_target_pairs={{8,256},{9,257},{10,258},{11,259},{12,260},{13,261},{14,262},{15,2... | collective-permute-start | bytes 786440 | tf_op jit(solution)/shard_map/ppermute | solution.py:152
  126.9 1.9 collective-permute-start.9
  128.8 4.3 %all-to-all-start.2 = ((bf16[8,128,256]{2,1,0:T(8,128)(2,1)}), bf16[8,128,256]{2,1,0:T(8,128)(2,1)}, u32[]{:S(2)}, u32[]{:S(2)}) async-start(bf16[8,128,256]{2,1,0:T(8,128)(2,1)} %bitcast.43), calls=%async_computation.2 | async-start | bytes 1048576 | tf_op jit(solution)/shard_map/all_to_all | solution.py:209
  133.1 15.6 %collective-permute-done.7 = bf16[512,256]{1,0:T(8,128)(2,1)} collective-permute-done((bf16[512,256]{1,0:T(8,128)(2,1)}, bf16[512,256]{1,0:T(8,128)(2,1)}, u32[]{:S(2)}, u32[]{:S(2)}) %collective-permute-start.7) | collective-permute-done | bytes 262176 | tf_op jit(solution)/shard_map/ppermute | solution.py:152
  148.7 1.9 collective-permute-start.8
  150.6 3.9 %collective-permute-done.9 = bf16[512,256]{1,0:T(8,128)(2,1)} collective-permute-done((bf16[512,256]{1,0:T(8,128)(2,1)S(1)}, bf16[512,256]{1,0:T(8,128)(2,1)}, u32[]{:S(2)}, u32[]{:S(2)}) %collective-permute-start.9) | collective-permute-done | bytes 262176 | tf_op jit(solution)/shard_map/ppermute | solution.py:152
  154.6 10.4 %collective-permute-start.10 = (bf16[512,256]{1,0:T(8,128)(2,1)}, bf16[512,256]{1,0:T(8,128)(2,1)S(1)}, u32[]{:S(2)}, u32[]{:S(2)}) collective-permute-start(bf16[512,256]{1,0:T(8,128)(2,1)} %collective-permute-done.9), channel_id=1, source_target_pairs={{264,0},{265,1},{266,2},{267,3},{268,4},{269,5},{270,6},{271,7},{3... | collective-permute-start | bytes 786440 | tf_op jit(solution)/shard_map/ppermute | solution.py:152
  165.0 1.3 fusion
  166.4 10.4 %collective-permute-done.8 = bf16[512,256]{1,0:T(8,128)(2,1)S(1)} collective-permute-done((bf16[512,256]{1,0:T(8,128)(2,1)}, bf16[512,256]{1,0:T(8,128)(2,1)S(1)}, u32[]{:S(2)}, u32[]{:S(2)}) %collective-permute-start.8) | collective-permute-done | bytes 262176 | tf_op jit(solution)/shard_map/ppermute | solution.py:152
  176.8 0.8 pad_maximum_fusion.5.back_ref
  177.6 3.2 %finish.1 = bf16[1024,256]{1,0:T(8,128)(2,1)} custom-call(f32[1024,256]{1,0:T(8,128)} %get-tuple-element.7.own_ref, bf16[1024,256]{1,0:T(8,128)(2,1)} %pad_maximum_fusion.5.back_ref, bf16[1024,256]{1,0:T(8,128)(2,1)} %bitcast.35, f32[2,128]{1,0:T(2,128)} %add.28.gain_ref, f32[1024,128]{1,0:T(8,128)} %get-tuple-element.25.cos_ref, ...), custom_call_target="tpu_custom_call" | custom-call | tf_op jit(solution)/shard_map/finish/pallas_call | solution.py:210
  180.8 8.3 %all-to-all-start.3 = ((bf16[8,128,256]{2,1,0:T(8,128)(2,1)}), bf16[8,128,256]{2,1,0:T(8,128)(2,1)S(1)}, u32[]{:S(2)}, u32[]{:S(2)}) async-start(bf16[8,128,256]{2,1,0:T(8,128)(2,1)} %bitcast.36), calls=%async_computation.3 | async-start | bytes 1048576 | tf_op jit(solution)/shard_map/all_to_all | solution.py:217
  189.1 1.3 copy.13
  190.5 1.0 reshape.48
  191.5 8.0 %all-to-all-done.3 = bf16[8,128,256]{2,1,0:T(8,128)(2,1)S(1)} async-done(((bf16[8,128,256]{2,1,0:T(8,128)(2,1)}), bf16[8,128,256]{2,1,0:T(8,128)(2,1)S(1)}, u32[]{:S(2)}, u32[]{:S(2)}) %all-to-all-start.3) | async-done | bytes 524320 | tf_op jit(solution)/shard_map/all_to_all | solution.py:217
  199.5 0.1 slice_bitcast_fusion
  199.6 0.2 copy.15
  199.7 0.8 reshape.51
  200.6 0.2 copy.14
  200.7 0.8 reshape.50
  (25 shorter events, 0.3 us)
Async XLA Ops:
  1.5 13.1 %collective-permute-start.4 = (f32[2,128]{1,0:T(2,128)S(1)}, f32[2,128]{1,0:T(2,128)S(1)}, u32[]{:S(2)}, u32[]{:S(2)}) collective-permute-start(f32[2,128]{1,0:T(2,128)S(1)} %dynamic_update_slice.5), channel_id=1, source_target_pairs={{0,64},{64,0},{128,192},{192,128},{256,320},{320,256},{384,448},{4... | collective-permute-start | bytes 3080 | tf_op jit(solution)/shard_map/ppermute | solution.py:177
  7.5 5.5 %copy-start.1 = (bf16[1,128,2048]{2,1,0:T(8,128)(2,1)S(1)}, bf16[1,128,2048]{2,1,0:T(8,128)(2,1)}, u32[]{:S(2)}) copy-start(bf16[1,128,2048]{2,1,0:T(8,128)(2,1)} %param.6) | copy-start | bytes 1572868
  8.4 4.7 %copy-start.2 = (bf16[1,128,2048]{2,1,0:T(8,128)(2,1)S(1)}, bf16[1,128,2048]{2,1,0:T(8,128)(2,1)}, u32[]{:S(2)}) copy-start(bf16[1,128,2048]{2,1,0:T(8,128)(2,1)} %param.9) | copy-start | bytes 1572868
  8.4 15.0 %all-to-all-start.1 = ((bf16[8,128,256]{2,1,0:T(8,128)(2,1)}), bf16[8,128,256]{2,1,0:T(8,128)(2,1)S(1)}, u32[]{:S(2)}, u32[]{:S(2)}) async-start(bf16[8,128,256]{2,1,0:T(8,128)(2,1)} %pad_maximum_fusion.3), calls=%async_computation.1 | async-start | bytes 1048576 | tf_op jit(solution)/shard_map/all_to_all | solution.py:166
  13.5 1.1 copy-start.3
  13.5 1.1 copy-start.4
  14.8 30.4 %collective-permute-start.5 = (f32[2,128]{1,0:T(2,128)S(1)}, f32[2,128]{1,0:T(2,128)S(1)}, u32[]{:S(2)}, u32[]{:S(2)}) collective-permute-start(f32[2,128]{1,0:T(2,128)S(1)} %add.26), channel_id=1, source_target_pairs={{0,128},{64,192},{128,0},{192,64},{256,384},{320,448},{384,256},{4... | collective-permute-start | bytes 3080 | tf_op jit(solution)/shard_map/ppermute | solution.py:177
  23.3 4.3 %copy-start = (bf16[8,128,256]{2,1,0:T(8,128)(2,1)}, bf16[8,128,256]{2,1,0:T(8,128)(2,1)S(1)}, u32[]{:S(2)}) copy-start(bf16[8,128,256]{2,1,0:T(8,128)(2,1)S(1)} %all-to-all-done.1) | copy-start | bytes 1572868
  23.3 70.3 %all-to-all-start = ((bf16[8,128,512]{2,1,0:T(8,128)(2,1)}), bf16[8,128,512]{2,1,0:T(8,128)(2,1)}, u32[]{:S(2)}, u32[]{:S(2)}) async-start(bf16[8,128,512]{2,1,0:T(8,128)(2,1)} %pad_maximum_fusion), calls=%async_computation | async-start | bytes 2097152 | tf_op jit(solution)/shard_map/all_to_all | solution.py:169
  27.6 32.6 %collective-permute-start.2 = (bf16[512,256]{1,0:T(8,128)(2,1)S(1)}, bf16[512,256]{1,0:T(8,128)(2,1)}, u32[]{:S(2)}, u32[]{:S(2)}) collective-permute-start(bf16[512,256]{1,0:T(8,128)(2,1)S(1)} %bitcast.47), channel_id=1, source_target_pairs={{0,264},{1,265},{2,266},{3,267},{4,268},{5,269},{6,270},{7,271},{6... | collective-permute-start | bytes 786440 | tf_op jit(solution)/shard_map/ppermute | solution.py:152
  39.5 27.9 %collective-permute-start = (bf16[512,256]{1,0:T(8,128)(2,1)S(1)}, bf16[512,256]{1,0:T(8,128)(2,1)}, u32[]{:S(2)}, u32[]{:S(2)}) collective-permute-start(bf16[512,256]{1,0:T(8,128)(2,1)S(1)} %bitcast.46), channel_id=1, source_target_pairs={{0,256},{1,257},{2,258},{3,259},{4,260},{5,261},{6,262},{7,263},{6... | collective-permute-start | bytes 786440 | tf_op jit(solution)/shard_map/ppermute | solution.py:152
  45.2 26.1 %collective-permute-start.6 = (f32[2,128]{1,0:T(2,128)S(1)}, f32[2,128]{1,0:T(2,128)S(1)}, u32[]{:S(2)}, u32[]{:S(2)}) collective-permute-start(f32[2,128]{1,0:T(2,128)S(1)} %add.27), channel_id=1, source_target_pairs={{0,256},{64,320},{128,384},{192,448},{256,0},{320,64},{384,128},{4... | collective-permute-start | bytes 3080 | tf_op jit(solution)/shard_map/ppermute | solution.py:177
  60.3 31.6 %collective-permute-start.3 = (bf16[512,256]{1,0:T(8,128)(2,1)}, bf16[512,256]{1,0:T(8,128)(2,1)S(1)}, u32[]{:S(2)}, u32[]{:S(2)}) collective-permute-start(bf16[512,256]{1,0:T(8,128)(2,1)} %collective-permute-done.2), channel_id=1, source_target_pairs={{264,8},{265,9},{266,10},{267,11},{268,12},{269,13},{270,14},{271,... | collective-permute-start | bytes 786440 | tf_op jit(solution)/shard_map/ppermute | solution.py:152
  67.4 24.5 %collective-permute-start.1 = (bf16[512,256]{1,0:T(8,128)(2,1)}, bf16[512,256]{1,0:T(8,128)(2,1)}, u32[]{:S(2)}, u32[]{:S(2)}) collective-permute-start(bf16[512,256]{1,0:T(8,128)(2,1)} %collective-permute-done), channel_id=1, source_target_pairs={{256,8},{257,9},{258,10},{259,11},{260,12},{261,13},{262,14},{263,... | collective-permute-start | bytes 786440 | tf_op jit(solution)/shard_map/ppermute | solution.py:152
  115.4 33.3 %collective-permute-start.7 = (bf16[512,256]{1,0:T(8,128)(2,1)}, bf16[512,256]{1,0:T(8,128)(2,1)}, u32[]{:S(2)}, u32[]{:S(2)}) collective-permute-start(bf16[512,256]{1,0:T(8,128)(2,1)} %get-tuple-element.11), channel_id=1, source_target_pairs={{8,256},{9,257},{10,258},{11,259},{12,260},{13,261},{14,262},{15,2... | collective-permute-start | bytes 786440 | tf_op jit(solution)/shard_map/ppermute | solution.py:152
  126.9 27.7 %collective-permute-start.9 = (bf16[512,256]{1,0:T(8,128)(2,1)S(1)}, bf16[512,256]{1,0:T(8,128)(2,1)}, u32[]{:S(2)}, u32[]{:S(2)}) collective-permute-start(bf16[512,256]{1,0:T(8,128)(2,1)S(1)} %get-tuple-element.12), channel_id=1, source_target_pairs={{8,264},{9,265},{10,266},{11,267},{12,268},{13,269},{14,270},{15,2... | collective-permute-start | bytes 786440 | tf_op jit(solution)/shard_map/ppermute | solution.py:152
  128.8 52.0 %all-to-all-start.2 = ((bf16[8,128,256]{2,1,0:T(8,128)(2,1)}), bf16[8,128,256]{2,1,0:T(8,128)(2,1)}, u32[]{:S(2)}, u32[]{:S(2)}) async-start(bf16[8,128,256]{2,1,0:T(8,128)(2,1)} %bitcast.43), calls=%async_computation.2 | async-start | bytes 1048576 | tf_op jit(solution)/shard_map/all_to_all | solution.py:209
  148.7 28.1 %collective-permute-start.8 = (bf16[512,256]{1,0:T(8,128)(2,1)}, bf16[512,256]{1,0:T(8,128)(2,1)S(1)}, u32[]{:S(2)}, u32[]{:S(2)}) collective-permute-start(bf16[512,256]{1,0:T(8,128)(2,1)} %collective-permute-done.7), channel_id=1, source_target_pairs={{256,0},{257,1},{258,2},{259,3},{260,4},{261,5},{262,6},{263,7},{3... | collective-permute-start | bytes 786440 | tf_op jit(solution)/shard_map/ppermute | solution.py:152
  154.6 22.2 %collective-permute-start.10 = (bf16[512,256]{1,0:T(8,128)(2,1)}, bf16[512,256]{1,0:T(8,128)(2,1)S(1)}, u32[]{:S(2)}, u32[]{:S(2)}) collective-permute-start(bf16[512,256]{1,0:T(8,128)(2,1)} %collective-permute-done.9), channel_id=1, source_target_pairs={{264,0},{265,1},{266,2},{267,3},{268,4},{269,5},{270,6},{271,7},{3... | collective-permute-start | bytes 786440 | tf_op jit(solution)/shard_map/ppermute | solution.py:152
  180.8 18.6 %all-to-all-start.3 = ((bf16[8,128,256]{2,1,0:T(8,128)(2,1)}), bf16[8,128,256]{2,1,0:T(8,128)(2,1)S(1)}, u32[]{:S(2)}, u32[]{:S(2)}) async-start(bf16[8,128,256]{2,1,0:T(8,128)(2,1)} %bitcast.36), calls=%async_computation.3 | async-start | bytes 1048576 | tf_op jit(solution)/shard_map/all_to_all | solution.py:217

commit v2 on v1

v2 whole, which is shorter than its diff:
```python
import functools

import jax
import jax.numpy as jnp
import numpy as np
from jax import lax
from jax.experimental import pallas as pl
from jax.experimental.pallas import tpu as pltpu
from jax.sharding import PartitionSpec as P

HEAD = 128
GROUP = 8
TOK = 128
SPAN = GROUP * TOK
WINDOW = 1024
SCALE = 168.0 ** (-0.5)
LOG2E = 1.4426950408889634
ROPE_BASE = 10000.0
EPSILON = 1e-06
NT = (((1,), (1,)), ((), ()))
NN = (((1,), (0,)), ((), ()))
MESH = pl.DeviceIdType.MESH
BF16 = jnp.bfloat16
F32 = jnp.float32


def mm(a, b, dims):
    return lax.dot_general(a, b, dims, preferred_element_type=F32)


def inverse_norm(x):
    return lax.rsqrt(jnp.mean(x * x, axis=-1, keepdims=True) + EPSILON)


def prepare(x, gain, cosine, sine):
    n = x * inverse_norm(x) * gain
    return n * cosine + pltpu.roll(n, HEAD // 2, 1) * sine


def prepare_back(x, gain, cosine, sine, dy):
    inv = inverse_norm(x)
    h = (dy * cosine + pltpu.roll(dy * sine, HEAD // 2, 1)) * gain
    return inv * h - x * (inv * inv * inv * jnp.mean(x * h, axis=-1, keepdims=True))


def block(i, base=0):
    return pl.ds(pl.multiple_of(base + i * TOK, TOK), TOK)


def lanes(i, width):
    return pl.ds(pl.multiple_of(i * width, width), width)


def layer_kernel(
    q_in, k_in, v_in, do_in, gain_in, cos_in, sin_in,
    oq, ok, ov,
    land, qd, gain_s, cos_s, sin_s, k_s, kt_s, dk_s, dv_s,
    relay_f, relay_b, ret_s, ret_l, qg_s, kvg_s, lq, lk, lv,
    in_send, in_recv, gain_send, gain_recv, z_send, z_recv, out_send, out_recv, self_sem,
):
    d = lax.axis_index("dp")
    seq = lax.axis_index("seq")
    r = lax.rem(seq, GROUP)
    g = lax.div(seq, GROUP)
    n_g = lax.div(lax.axis_size("seq"), GROUP)
    n_x = n_g // 2
    x = lax.div(g, 2)
    z = lax.rem(g, 2) * 8 + d
    low = jnp.where(g == 0, SPAN, 0)

    def mate(p):
        return (d, g * GROUP + p)

    def place(px, pz):
        return (lax.rem(pz, 8), (px * 2 + lax.div(pz, 8)) * GROUP + r)

    def up(sign):
        return lax.rem(z + 4 * sign + 16, 16)

    def remote(src, dst, send, recv, device):
        return pltpu.make_async_remote_copy(
            src_ref=src, dst_ref=dst, send_sem=send, recv_sem=recv, device_id=device, device_id_type=MESH
        )

    barrier = pltpu.get_barrier_semaphore()

    def greet(device):
        pl.semaphore_signal(barrier, inc=1, device_id=device, device_id_type=MESH)

    for k in range(1, GROUP):
        greet(mate(lax.rem(r + k, GROUP)))
    for k in range(1, 8):
        greet((lax.rem(d + k, 8), seq))
    for dx in (-1, 0, 1):
        for hi in (0, 1):
            greet((lax.rem(d + 4, 8), (lax.rem(x + dx + n_x, n_x) * 2 + hi) * GROUP + r))
    pl.semaphore_wait(barrier, 20)

    kinds = (
        (k_in, HEAD, land, SPAN, 0),
        (v_in, HEAD, land, SPAN, HEAD),
        (q_in, 2 * HEAD, qd, 0, 0),
        (do_in, 2 * HEAD, qd, 0, 2 * HEAD),
    )

    def into(kind, k):
        src, width, dst, base, at = kinds[kind]
        p = lax.rem(r + k, GROUP)
        return remote(
            src.at[0, :, lanes(p, width)], dst.at[block(r, base), at : at + width],
            in_send.at[kind, k], in_recv.at[kind, k], mate(p),
        )

    def keep(kind):
        src, width, dst, base, at = kinds[kind]
        return pltpu.make_async_copy(
            src.at[0, :, lanes(r, width)], dst.at[block(r, base), at : at + width], self_sem.at[kind]
        )

    def share(k):
        return remote(
            gain_in, gain_s.at[k], gain_send.at[k], gain_recv.at[k], (lax.rem(d + k, 8), seq)
        )

    for kind in (0, 1):
        keep(kind).start()
    for k in range(1, GROUP):
        for kind in (0, 1):
            into(kind, k).start()
    for k in range(1, 8):
        share(k).start()
    for kind in (2, 3):
        keep(kind).start()
    for k in range(1, GROUP):
        for kind in (2, 3):
            into(kind, k).start()

    def chunk(c):
        return lax.rem(r - c + GROUP, GROUP)

    def leg0(c):
        return remote(
            land.at[block(chunk(c), SPAN), :], relay_f.at[c],
            z_send.at[0, c], z_recv.at[0, c], place(x, up(1 - 2 * (c % 2))),
        )

    def leg1(c):
        sign = 1 - 2 * (c % 2)
        return remote(
            relay_f.at[c], land.at[block(chunk(c)), :],
            z_send.at[1, c], z_recv.at[1, c],
            place(lax.rem(x + lax.div(up(-sign), 8), n_x), up(sign)),
        )

    def leg2(c):
        sign = 1 - 2 * (c % 2)
        return remote(
            ret_s.at[block(c), :], relay_b.at[c],
            z_send.at[2, c], z_recv.at[2, c],
            place(lax.rem(x + n_x - 1 + lax.div(z, 8), n_x), up(-sign)),
        )

    def leg3(c):
        sign = 1 - 2 * (c % 2)
        return remote(
            relay_b.at[c], ret_l.at[block(c), :],
            z_send.at[3, c], z_recv.at[3, c], place(x, up(-sign)),
        )

    for c in range(GROUP):
        for kind in (0, 1):
            if c == 0:
                keep(kind).wait()
            else:
                into(kind, c).wait_recv()
        leg0(c).start()

    gains = gain_in[...]
    for k in range(1, 8):
        share(k).wait_recv()
        gains = gains + gain_s[k]
    q_gain, k_gain = gains[0:1, :], gains[1:2, :]

    def hat(at):
        raw = land[at, :HEAD].astype(F32)
        key = prepare(raw, k_gain, cos_s[at, :], sin_s[at, :])
        k_s[at, :] = key.astype(BF16)
        kt_s[:, at] = key.T.astype(BF16)

    cos_t, sin_t = cos_in[16:, :], sin_in[16:, :]

    def tables(i, _):
        cos_b, sin_b = cos_in[pl.ds(i, 1), :], sin_in[pl.ds(i, 1), :]
        cos_s[block(i), :] = cos_b * cos_t - sin_b * sin_t
        sin_s[block(i), :] = sin_b * cos_t + cos_b * sin_t
        dk_s[block(i), :] = jnp.zeros((TOK, HEAD), F32)
        dv_s[block(i), :] = jnp.zeros((TOK, HEAD), F32)
        return 0

    lax.fori_loop(0, 2 * GROUP, tables, 0)

    def own_keys(i, _):
        hat(block(i, SPAN))
        return 0

    lax.fori_loop(0, GROUP, own_keys, 0)

    for c in range(GROUP):
        leg0(c).wait_recv()
        leg1(c).start()
    for kind in (2, 3):
        keep(kind).wait()
        for k in range(1, GROUP):
            into(kind, k).wait_recv()

    def previous_keys(c, _):
        leg1(c).wait_recv()
        hat(block(chunk(c)))
        return 0

    lax.fori_loop(0, GROUP, previous_keys, 0)

    outs = ((qg_s, 0, 2 * HEAD, lq), (kvg_s, 0, HEAD, lk), (kvg_s, HEAD, HEAD, lv))

    def send_out(kind, p):
        src, at, width, dst = outs[kind]
        return remote(
            src.at[block(p), at : at + width], dst.at[:, lanes(r, width)],
            out_send.at[kind, p], out_recv.at[kind, r], mate(p),
        )

    def keep_out(kind):
        src, at, width, dst = outs[kind]
        return pltpu.make_async_copy(
            src.at[block(r), at : at + width], dst.at[:, lanes(r, width)], self_sem.at[4 + kind]
        )

    def arrive_out(kind, p):
        src, at, width, dst = outs[kind]
        return remote(
            src.at[block(p), at : at + width], dst.at[:, lanes(p, width)],
            out_send.at[kind, p], out_recv.at[kind, p], mate(p),
        )

    def deliver(kind, p):
        @pl.when(p != r)
        def _():
            send_out(kind, p).start()

        @pl.when(p == r)
        def _():
            keep_out(kind).start()

    wide = WINDOW + TOK

    def step(b, _):
        rows, keys = block(b), pl.ds(pl.multiple_of(b * TOK, TOK), wide)
        cosine, sine = cos_s[block(b, SPAN), :], sin_s[block(b, SPAN), :]
        raw = [qd[rows, h * HEAD : (h + 1) * HEAD].astype(F32) for h in range(2)]
        q = jnp.concatenate([prepare(v, q_gain, cosine, sine) for v in raw], axis=0).astype(BF16)
        do = jnp.concatenate([qd[rows, (2 + h) * HEAD : (3 + h) * HEAD] for h in range(2)], axis=0)
        s = mm(k_s[keys, :], q, NT)
        row = lax.broadcasted_iota(jnp.int32, (wide, 2 * TOK), 0)
        col = lax.broadcasted_iota(jnp.int32, (wide, 2 * TOK), 1) % TOK
        seen = (row > col) & (row <= col + WINDOW) & (row >= low - b * TOK)
        s = jnp.where(seen, s * (SCALE * LOG2E), -1e30)
        w = jnp.exp2(s - jnp.max(s, axis=0, keepdims=True))
        probs = w * (1.0 / jnp.sum(w, axis=0, keepdims=True))
        pb = probs.astype(BF16)
        dp = mm(land[keys, HEAD:], do, NT)
        delta = jnp.sum(pb.astype(F32) * dp, axis=0, keepdims=True)
        ds = (probs * (dp - delta)).astype(BF16)
        dv_s[keys, :] += mm(pb, do, NN)
        dk_s[keys, :] += mm(ds, q, NN)
        ret_s[rows, :HEAD] = (dk_s[rows, :] * SCALE).astype(BF16)
        ret_s[rows, HEAD:] = dv_s[rows, :].astype(BF16)
        leg2(b).start()
        dq = (mm(kt_s[:, keys], ds, NN) * SCALE).T
        for h in range(2):
            back = prepare_back(raw[h], q_gain, cosine, sine, dq[h * TOK : (h + 1) * TOK, :])
            qg_s[rows, h * HEAD : (h + 1) * HEAD] = back.astype(BF16)

        @pl.when(b >= 2)
        def _():
            leg2(b - 2).wait_recv()
            leg3(b - 2).start()

        deliver(0, b)
        return 0

    lax.fori_loop(0, GROUP, step, 0)
    for c in (GROUP - 2, GROUP - 1):
        leg2(c).wait_recv()
        leg3(c).start()

    def finish(b, _):
        rows, at = block(b), block(b, SPAN)
        leg3(b).wait_recv()
        dk = dk_s[at, :] * SCALE + ret_l[rows, :HEAD].astype(F32)
        back = prepare_back(land[at, :HEAD].astype(F32), k_gain, cos_s[at, :], sin_s[at, :], dk)
        kvg_s[rows, :HEAD] = back.astype(BF16)
        kvg_s[rows, HEAD:] = (dv_s[at, :] + ret_l[rows, HEAD:].astype(F32)).astype(BF16)
        deliver(1, b)
        deliver(2, b)
        return 0

    lax.fori_loop(0, GROUP, finish, 0)

    for k in range(1, GROUP):
        for kind in range(4):
            into(kind, k).wait_send()
        share(k).wait_send()
    for c in range(GROUP):
        for leg in (leg0, leg1, leg2, leg3):
            leg(c).wait_send()
    for kind, result in ((0, oq), (1, ok), (2, ov)):
        for k in range(1, GROUP):
            p = lax.rem(r + k, GROUP)
            arrive_out(kind, p).wait_recv()
            send_out(kind, p).wait_send()
        keep_out(kind).wait()
        result[0] = outs[kind][3][...]


def body(queries, raw_key_rows, values, out_grad, query_gain, key_norm_gain):
    dp = lax.axis_index("dp")
    part = jnp.stack([query_gain, key_norm_gain])
    gains = lax.dynamic_update_slice(jnp.zeros((8, HEAD), F32), part, (0, dp * part.shape[1]))
    group = lax.axis_index("seq") // GROUP
    index = jnp.arange(16 + TOK, dtype=jnp.int32)
    positions = jnp.where(index < 16, (group - 1) * SPAN + index * TOK, index - 16).astype(F32)
    half = np.arange(HEAD) % (HEAD // 2)
    frequency = jnp.asarray((ROPE_BASE ** (-half * (2.0 / HEAD))).astype(np.float32))
    sign = jnp.asarray(np.where(np.arange(HEAD) < HEAD // 2, -1.0, 1.0).astype(np.float32))
    angles = positions[:, None] * frequency[None, :]
    anywhere = pl.BlockSpec(memory_space=pl.ANY)
    vmem = pl.BlockSpec(memory_space=pltpu.VMEM)
    dma = pltpu.SemaphoreType.DMA
    return pl.pallas_call(
        layer_kernel,
        out_shape=tuple(
            jax.ShapeDtypeStruct(a.shape, BF16) for a in (queries, raw_key_rows, values)
        ),
        in_specs=[anywhere] * 4 + [vmem] * 3,
        out_specs=(vmem, vmem, vmem),
        scratch_shapes=[
            pltpu.VMEM((2 * SPAN, 2 * HEAD), BF16),
            pltpu.VMEM((SPAN, 4 * HEAD), BF16),
            pltpu.VMEM((8, 8, HEAD), F32),
            pltpu.VMEM((2 * SPAN, HEAD), F32),
            pltpu.VMEM((2 * SPAN, HEAD), F32),
            pltpu.VMEM((2 * SPAN, HEAD), BF16),
            pltpu.VMEM((HEAD, 2 * SPAN), BF16),
            pltpu.VMEM((2 * SPAN, HEAD), F32),
            pltpu.VMEM((2 * SPAN, HEAD), F32),
            pltpu.VMEM((GROUP, TOK, 2 * HEAD), BF16),
            pltpu.VMEM((GROUP, TOK, 2 * HEAD), BF16),
            pltpu.VMEM((SPAN, 2 * HEAD), BF16),
            pltpu.VMEM((SPAN, 2 * HEAD), BF16),
            pltpu.VMEM((SPAN, 2 * HEAD), BF16),
            pltpu.VMEM((SPAN, 2 * HEAD), BF16),
            pltpu.VMEM((TOK, 2 * SPAN), BF16),
            pltpu.VMEM((TOK, SPAN), BF16),
            pltpu.VMEM((TOK, SPAN), BF16),
            dma((4, 8)), dma((4, 8)), dma((8,)), dma((8,)),
            dma((4, 8)), dma((4, 8)), dma((3, 8)), dma((3, 8)), dma((7,)),
        ],
        compiler_params=pltpu.CompilerParams(collective_id=0, has_side_effects=True),
        name="layer_backward",
    )(
        queries, raw_key_rows, values, out_grad, gains,
        jnp.cos(angles), jnp.sin(angles) * sign[None, :],
    )


def solution(mesh):
    spec = P("dp", "seq", None)
    return jax.shard_map(
        body,
        mesh=mesh,
        in_specs=(spec, spec, spec, spec, P("dp"), P("dp")),
        out_specs=(spec, spec, spec),
        check_vma=False,
    )
```

time: 202 us -> 136 us (0.67)
  the two profiles are of different devices: /device:TPU:4 before, /device:TPU:25 now
where the time goes in v2:
time: 136 us
  Pallas kernels  129 us (95%)
  local copies, waits for them, and re-layouts  4.97 us (4%)
    pallas_call x1, Pallas kernels, body(): pl.pallas_call(layer_kernel, out_shape=tuple((jax.ShapeDtypeStruct(a.shap...  129 us
    unnamed x17, local copies, waits for them, and re-layouts  4.65 us

profile of v2, /device:TPU:25, one launch (start us, length us, event | category | flops | bytes accessed | tf_op | source)
XLA Modules:
  0.0 135.6 jit_solution(9307982892858213823)
XLA Ops:
  0.6 0.0 copy-start.5
  0.7 0.0 copy-start.6
  0.7 0.6 copy-done.5
  1.3 0.0 copy-done.6
  1.3 0.0 copy-start.3
  1.3 0.0 copy-start.4
  1.4 0.3 dynamic_update_slice.3.gain_in
  1.7 0.3 copy-done.3
  2.0 0.0 copy-done.4
  2.0 0.0 copy-start.2
  2.0 1.0 fusion
  3.0 0.0 copy-done.2
  3.0 128.9 %layer_backward.1 = (bf16[1,128,2048]{2,1,0:T(8,128)(2,1)}, bf16[1,128,1024]{2,1,0:T(8,128)(2,1)}, bf16[1,128,1024]{2,1,0:T(8,128)(2,1)}) custom-call(bf16[1,128,2048]{2,1,0:T(8,128)(2,1)} %q_in.1, bf16[1,128,1024]{2,1,0:T(8,128)(2,1)} %k_in.1, bf16[1,128,1024]{2,1,0:T(8,128)(2,1)} %v_in.1, bf16[1,128,2048]{2,1,0:T(8,128)(2,1)} %do_in.1, ...), custom_call_target="tpu_custom_call" | custom-call | tf_op jit(solution)/shard_map/layer_backward/pallas_call | solution.py:339
  131.9 0.0 copy-start.1
  132.0 1.9 %copy.15 = bf16[1,128,2048]{2,1,0:T(8,128)(2,1)} copy(bf16[1,128,2048]{2,1,0:T(8,128)(2,1)} %get-tuple-element.8) | data formatting | bytes 1048576
  133.9 0.0 copy-done.1
  133.9 0.0 copy-start
  133.9 0.7 copy.16
  134.6 0.3 copy-done
  134.9 0.7 copy.17
  (3 shorter events, 0.0 us)
Async XLA Ops:
  0.6 0.7 copy-start.5
  0.7 0.7 copy-start.6
  1.3 0.7 copy-start.3
  1.3 0.7 copy-start.4
  2.0 1.0 copy-start.2
  131.9 1.9 %copy-start.1 = (bf16[1,128,1024]{2,1,0:T(8,128)(2,1)S(1)}, bf16[1,128,1024]{2,1,0:T(8,128)(2,1)}, u32[]{:S(2)}) copy-start(bf16[1,128,1024]{2,1,0:T(8,128)(2,1)} %get-tuple-element.9) | copy-start | bytes 786436
  133.9 1.0 copy-start

commit v3 on v2

--- a/solution.py
+++ b/solution.py
@@ -45,6 +45,10 @@
 
 def block(i, base=0):
     return pl.ds(pl.multiple_of(base + i * TOK, TOK), TOK)
+
+
+def half(i, s, base=0):
+    return pl.ds(pl.multiple_of(base + i * TOK + s * (TOK // 2), TOK // 2), TOK // 2)
 
 
 def lanes(i, width):
@@ -129,43 +133,39 @@
             into(kind, k).start()
     for k in range(1, 8):
         share(k).start()
-    for kind in (2, 3):
-        keep(kind).start()
-    for k in range(1, GROUP):
-        for kind in (2, 3):
-            into(kind, k).start()
-
     def chunk(c):
         return lax.rem(r - c + GROUP, GROUP)
 
-    def leg0(c):
-        return remote(
-            land.at[block(chunk(c), SPAN), :], relay_f.at[c],
-            z_send.at[0, c], z_recv.at[0, c], place(x, up(1 - 2 * (c % 2))),
-        )
-
-    def leg1(c):
-        sign = 1 - 2 * (c % 2)
-        return remote(
-            relay_f.at[c], land.at[block(chunk(c)), :],
-            z_send.at[1, c], z_recv.at[1, c],
-            place(lax.rem(x + lax.div(up(-sign), 8), n_x), up(sign)),
-        )
-
-    def leg2(c):
-        sign = 1 - 2 * (c % 2)
-        return remote(
-            ret_s.at[block(c), :], relay_b.at[c],
-            z_send.at[2, c], z_recv.at[2, c],
-            place(lax.rem(x + n_x - 1 + lax.div(z, 8), n_x), up(-sign)),
-        )
-
-    def leg3(c):
-        sign = 1 - 2 * (c % 2)
-        return remote(
-            relay_b.at[c], ret_l.at[block(c), :],
-            z_send.at[3, c], z_recv.at[3, c], place(x, up(-sign)),
-        )
+    def hop(leg, c, s, src, dst, device):
+        return remote(src, dst, z_send.at[leg, s, c], z_recv.at[leg, s, c], device)
+
+    def leg0(c, s):
+        return hop(0, c, s, land.at[half(chunk(c), s, SPAN), :], relay_f.at[half(c, s), :], place(x, up(1 - 2 * s)))
+
+    def leg1(c, s):
+        sign = 1 - 2 * s
+        to = place(lax.rem(x + lax.div(up(-sign), 8), n_x), up(sign))
+        return hop(1, c, s, relay_f.at[half(c, s), :], land.at[half(chunk(c), s), :], to)
+
+    def leg2(c, s):
+        to = place(lax.rem(x + n_x - 1 + lax.div(z, 8), n_x), up(2 * s - 1))
+        return hop(2, c, s, ret_s.at[half(c, s), :], relay_b.at[half(c, s), :], to)
+
+    def leg3(c, s):
+        return hop(3, c, s, relay_b.at[half(c, s), :], ret_l.at[half(c, s), :], place(x, up(2 * s - 1)))
+
+    def start(leg, c):
+        for s in (0, 1):
+            leg(c, s).start()
+
+    def arrive(leg, c):
+        for s in (0, 1):
+            leg(c, s).wait_recv()
+
+    def forward(first, second, c):
+        for s in (0, 1):
+            first(c, s).wait_recv()
+            second(c, s).start()
 
     for c in range(GROUP):
         for kind in (0, 1):
@@ -173,7 +173,13 @@
                 keep(kind).wait()
             else:
                 into(kind, c).wait_recv()
-        leg0(c).start()
+        start(leg0, c)
+
+    for kind in (2, 3):
+        keep(kind).start()
+    for k in range(1, GROUP):
+        for kind in (2, 3):
+            into(kind, k).start()
 
     gains = gain_in[...]
     for k in range(1, 8):
@@ -189,32 +195,29 @@
 
     cos_t, sin_t = cos_in[16:, :], sin_in[16:, :]
 
-    def tables(i, _):
+    def table(at, i):
         cos_b, sin_b = cos_in[pl.ds(i, 1), :], sin_in[pl.ds(i, 1), :]
-        cos_s[block(i), :] = cos_b * cos_t - sin_b * sin_t
-        sin_s[block(i), :] = sin_b * cos_t + cos_b * sin_t
-        dk_s[block(i), :] = jnp.zeros((TOK, HEAD), F32)
-        dv_s[block(i), :] = jnp.zeros((TOK, HEAD), F32)
+        cos_s[at, :] = cos_b * cos_t - sin_b * sin_t
+        sin_s[at, :] = sin_b * cos_t + cos_b * sin_t
+        dk_s[at, :] = jnp.zeros((TOK, HEAD), F32)
+        dv_s[at, :] = jnp.zeros((TOK, HEAD), F32)
+
+    def first_half(c, _):
+        forward(leg0, leg1, c)
+        table(block(c), c)
+        table(block(c, SPAN), c + GROUP)
+        hat(block(c, SPAN))
         return 0
 
-    lax.fori_loop(0, 2 * GROUP, tables, 0)
-
-    def own_keys(i, _):
-        hat(block(i, SPAN))
-        return 0
-
-    lax.fori_loop(0, GROUP, own_keys, 0)
-
-    for c in range(GROUP):
-        leg0(c).wait_recv()
-        leg1(c).start()
+    lax.fori_loop(0, GROUP, first_half, 0)
+
     for kind in (2, 3):
         keep(kind).wait()
         for k in range(1, GROUP):
             into(kind, k).wait_recv()
 
     def previous_keys(c, _):
-        leg1(c).wait_recv()
+        arrive(leg1, c)
         hat(block(chunk(c)))
         return 0
 
@@ -274,7 +277,7 @@
         dk_s[keys, :] += mm(ds, q, NN)
         ret_s[rows, :HEAD] = (dk_s[rows, :] * SCALE).astype(BF16)
         ret_s[rows, HEAD:] = dv_s[rows, :].astype(BF16)
-        leg2(b).start()
+        start(leg2, b)
         dq = (mm(kt_s[:, keys], ds, NN) * SCALE).T
         for h in range(2):
             back = prepare_back(raw[h], q_gain, cosine, sine, dq[h * TOK : (h + 1) * TOK, :])
@@ -282,20 +285,18 @@
 
         @pl.when(b >= 2)
         def _():
-            leg2(b - 2).wait_recv()
-            leg3(b - 2).start()
+            forward(leg2, leg3, b - 2)
 
         deliver(0, b)
         return 0
 
     lax.fori_loop(0, GROUP, step, 0)
     for c in (GROUP - 2, GROUP - 1):
-        leg2(c).wait_recv()
-        leg3(c).start()
+        forward(leg2, leg3, c)
 
     def finish(b, _):
         rows, at = block(b), block(b, SPAN)
-        leg3(b).wait_recv()
+        arrive(leg3, b)
         dk = dk_s[at, :] * SCALE + ret_l[rows, :HEAD].astype(F32)
         back = prepare_back(land[at, :HEAD].astype(F32), k_gain, cos_s[at, :], sin_s[at, :], dk)
         kvg_s[rows, :HEAD] = back.astype(BF16)
@@ -312,7 +313,8 @@
         share(k).wait_send()
     for c in range(GROUP):
         for leg in (leg0, leg1, leg2, leg3):
-            leg(c).wait_send()
+            for s in (0, 1):
+                leg(c, s).wait_send()
     for kind, result in ((0, oq), (1, ok), (2, ov)):
         for k in range(1, GROUP):
             p = lax.rem(r + k, GROUP)
@@ -320,6 +322,14 @@
             send_out(kind, p).wait_send()
         keep_out(kind).wait()
         result[0] = outs[kind][3][...]
+
+
+def settle_kernel(a, b, c, oa, ob, oc, sem):
+    copies = [pltpu.make_async_copy(i, o, sem.at[n]) for n, (i, o) in enumerate(((a, oa), (b, ob), (c, oc)))]
+    for copy in copies:
+        copy.start()
+    for copy in copies:
+        copy.wait()
 
 
 def body(queries, raw_key_rows, values, out_grad, query_gain, key_norm_gain):
@@ -336,11 +346,10 @@
     anywhere = pl.BlockSpec(memory_space=pl.ANY)
     vmem = pl.BlockSpec(memory_space=pltpu.VMEM)
     dma = pltpu.SemaphoreType.DMA
-    return pl.pallas_call(
+    shapes = tuple(jax.ShapeDtypeStruct(a.shape, BF16) for a in (queries, raw_key_rows, values))
+    grads = pl.pallas_call(
         layer_kernel,
-        out_shape=tuple(
-            jax.ShapeDtypeStruct(a.shape, BF16) for a in (queries, raw_key_rows, values)
-        ),
+        out_shape=shapes,
         in_specs=[anywhere] * 4 + [vmem] * 3,
         out_specs=(vmem, vmem, vmem),
         scratch_shapes=[
@@ -353,8 +362,8 @@
             pltpu.VMEM((HEAD, 2 * SPAN), BF16),
             pltpu.VMEM((2 * SPAN, HEAD), F32),
             pltpu.VMEM((2 * SPAN, HEAD), F32),
-            pltpu.VMEM((GROUP, TOK, 2 * HEAD), BF16),
-            pltpu.VMEM((GROUP, TOK, 2 * HEAD), BF16),
+            pltpu.VMEM((SPAN, 2 * HEAD), BF16),
+            pltpu.VMEM((SPAN, 2 * HEAD), BF16),
             pltpu.VMEM((SPAN, 2 * HEAD), BF16),
             pltpu.VMEM((SPAN, 2 * HEAD), BF16),
             pltpu.VMEM((SPAN, 2 * HEAD), BF16),
@@ -363,7 +372,7 @@
             pltpu.VMEM((TOK, SPAN), BF16),
             pltpu.VMEM((TOK, SPAN), BF16),
             dma((4, 8)), dma((4, 8)), dma((8,)), dma((8,)),
-            dma((4, 8)), dma((4, 8)), dma((3, 8)), dma((3, 8)), dma((7,)),
+            dma((4, 2, 8)), dma((4, 2, 8)), dma((3, 8)), dma((3, 8)), dma((7,)),
         ],
         compiler_params=pltpu.CompilerParams(collective_id=0, has_side_effects=True),
         name="layer_backward",
@@ -371,6 +380,14 @@
         queries, raw_key_rows, values, out_grad, gains,
         jnp.cos(angles), jnp.sin(angles) * sign[None, :],
     )
+    return pl.pallas_call(
+        settle_kernel,
+        out_shape=shapes,
+        in_specs=[vmem] * 3,
+        out_specs=(anywhere,) * 3,
+        scratch_shapes=[dma((3,))],
+        name="settle",
+    )(*grads)
 
 
 def solution(mesh):

time: 136 us -> 130 us (0.956)
  local copies, waits for them, and re-layouts: 4.97 us -> 1.3 us
  Pallas kernels: 129 us -> 126 us
    unnamed x17 -> x10, local copies, waits for them, and re-layouts: 4.65 us -> 0.98 us
    pallas_call x1 -> x2, Pallas kernels: 129 us -> 126 us  [the longest x1 124 us: body(): pl.pallas_call(layer_kernel, out_shape=shapes, in_specs=[anywhere] * 4 +...]
where the time goes in v3:
time: 130 us; the launch traced here: 129 us
  Pallas kernels  126 us (97%)
  local copies, waits for them, and re-layouts  1.3 us (1%)
    pallas_call x1, Pallas kernels, body(): pl.pallas_call(layer_kernel, out_shape=shapes, in_specs=[anywhere] * 4 +...  124 us

profile of v3, /device:TPU:25, one launch (start us, length us, event | category | flops | bytes accessed | tf_op | source)
XLA Modules:
  0.0 129.1 jit_solution(12409913289165320322)
XLA Ops:
  0.6 0.0 copy-start.3
  0.7 0.0 copy-start.4
  0.7 0.6 copy-done.3
  1.3 0.0 copy-done.4
  1.3 0.0 copy-start.1
  1.3 0.0 copy-start.2
  1.4 0.3 dynamic_update_slice.3.gain_in
  1.7 0.3 copy-done.1
  2.0 0.0 copy-done.2
  2.0 0.0 copy-start
  2.0 1.0 fusion
  3.0 0.0 copy-done
  3.0 123.9 %layer_backward.1 = (bf16[1,128,2048]{2,1,0:T(8,128)(2,1)}, bf16[1,128,1024]{2,1,0:T(8,128)(2,1)}, bf16[1,128,1024]{2,1,0:T(8,128)(2,1)}) custom-call(bf16[1,128,2048]{2,1,0:T(8,128)(2,1)} %q_in.1, bf16[1,128,1024]{2,1,0:T(8,128)(2,1)} %k_in.1, bf16[1,128,1024]{2,1,0:T(8,128)(2,1)} %v_in.1, bf16[1,128,2048]{2,1,0:T(8,128)(2,1)} %do_in.1, f32[8,128]{1,0:T(8,128)} %copy-done, ...), custom_call_target="tpu_custom_call" | custom-call | tf_op jit(solution)/shard_map/layer_backward/pallas_call | solution.py:350
  127.0 2.2 %settle.1 = (bf16[1,128,2048]{2,1,0:T(8,128)(2,1)}, bf16[1,128,1024]{2,1,0:T(8,128)(2,1)}, bf16[1,128,1024]{2,1,0:T(8,128)(2,1)}) custom-call(bf16[1,128,2048]{2,1,0:T(8,128)(2,1)} %get-tuple-element.6.a, bf16[1,128,1024]{2,1,0:T(8,128)(2,1)} %get-tuple-element.7.b, bf16[1,128,1024]{2,1,0:T(8,128)(2,1)} %get-tuple-element.8.c), custom_call_target="tpu_custom_call" | custom-call | tf_op jit(solution)/shard_map/settle/pallas_call | solution.py:383
  (3 shorter events, 0.0 us)
Async XLA Ops:
  0.6 0.7 copy-start.3
  0.7 0.7 copy-start.4
  1.3 0.7 copy-start.1
  1.3 0.7 copy-start.2
  2.0 1.0 copy-start

commit v4 on v3

--- a/solution.py
+++ b/solution.py
@@ -75,11 +75,15 @@
     def mate(p):
         return (d, g * GROUP + p)
 
+    out_far, back_far = 2 * n_x - 2 - 2 * x, 2 * x
+    has_next, has_previous = (z < 8) | (x < n_x - 1), g > 0
+    out_kind, back_kind = lax.div(z, 8), 1 - lax.div(z, 8)
+
+    def wrap(v):
+        return lax.rem(v + 32, 16)
+
     def place(px, pz):
-        return (lax.rem(pz, 8), (px * 2 + lax.div(pz, 8)) * GROUP + r)
-
-    def up(sign):
-        return lax.rem(z + 4 * sign + 16, 16)
+        return (lax.rem(pz, 8), (lax.rem(px + n_x, n_x) * 2 + lax.div(pz, 8)) * GROUP + r)
 
     def remote(src, dst, send, recv, device):
         return pltpu.make_async_remote_copy(
@@ -95,10 +99,22 @@
         greet(mate(lax.rem(r + k, GROUP)))
     for k in range(1, 8):
         greet((lax.rem(d + k, 8), seq))
-    for dx in (-1, 0, 1):
-        for hi in (0, 1):
-            greet((lax.rem(d + 4, 8), (lax.rem(x + dx + n_x, n_x) * 2 + hi) * GROUP + r))
-    pl.semaphore_wait(barrier, 20)
+    for sign in (1, -1):
+        greet(place(x, wrap(z + 4 * sign)))
+
+        @pl.when(x < n_x - 1)
+        def _():
+            greet(place(x, wrap(z + out_far * sign)))
+            greet(place(x + 1, wrap(z + out_far * sign)))
+            greet(place(x + 1, wrap(z + (2 * x + 2) * sign)))
+
+        @pl.when(x > 0)
+        def _():
+            greet(place(x, wrap(z + back_far * sign)))
+            greet(place(x - 1, wrap(z + (2 * n_x - 2 * x) * sign)))
+            greet(place(x - 1, wrap(z + back_far * sign)))
+
+    pl.semaphore_wait(barrier, 16 + 6 * jnp.where(x < n_x - 1, 1, 0) + 6 * jnp.where(x > 0, 1, 0))
 
     kinds = (
         (k_in, HEAD, land, SPAN, 0),
@@ -136,36 +152,64 @@
     def chunk(c):
         return lax.rem(r - c + GROUP, GROUP)
 
-    def hop(leg, c, s, src, dst, device):
-        return remote(src, dst, z_send.at[leg, s, c], z_recv.at[leg, s, c], device)
-
-    def leg0(c, s):
-        return hop(0, c, s, land.at[half(chunk(c), s, SPAN), :], relay_f.at[half(c, s), :], place(x, up(1 - 2 * s)))
-
-    def leg1(c, s):
+    def hop(leg, c, s, kind, end, src, dst, device):
+        mark = c if end else c + kind * GROUP
+        return remote(src, dst, z_send.at[leg, s, c + kind * GROUP], z_recv.at[leg, s, mark], device)
+
+    def leg0(c, s, kind):
+        to = place(x + kind, wrap(z + (4 + kind * (out_far - 4)) * (1 - 2 * s)))
+        held = relay_f.at[half(c + kind * GROUP, s), :]
+        return hop(0, c, s, kind, False, land.at[half(chunk(c), s, SPAN), :], held, to)
+
+    def leg1(c, s, kind):
         sign = 1 - 2 * s
-        to = place(lax.rem(x + lax.div(up(-sign), 8), n_x), up(sign))
-        return hop(1, c, s, relay_f.at[half(c, s), :], land.at[half(chunk(c), s), :], to)
-
-    def leg2(c, s):
-        to = place(lax.rem(x + n_x - 1 + lax.div(z, 8), n_x), up(2 * s - 1))
-        return hop(2, c, s, ret_s.at[half(c, s), :], relay_b.at[half(c, s), :], to)
-
-    def leg3(c, s):
-        return hop(3, c, s, relay_b.at[half(c, s), :], ret_l.at[half(c, s), :], place(x, up(2 * s - 1)))
-
-    def start(leg, c):
+        to = place(x, wrap(z + (back_far if kind else 4) * sign))
+        held = relay_f.at[half(c + kind * GROUP, s), :]
+        return hop(1, c, s, kind, True, held, land.at[half(chunk(c), s), :], to)
+
+    def leg2(c, s, kind):
+        to = place(x - kind, wrap(z - (4 + kind * (back_far - 4)) * (1 - 2 * s)))
+        held = relay_b.at[half(c + kind * GROUP, s), :]
+        return hop(2, c, s, kind, False, ret_s.at[half(c, s), :], held, to)
+
+    def leg3(c, s, kind):
+        sign = 1 - 2 * s
+        to = place(x, wrap(z - (out_far if kind else 4) * sign))
+        held = relay_b.at[half(c + kind * GROUP, s), :]
+        return hop(3, c, s, kind, True, held, ret_l.at[half(c, s), :], to)
+
+    def relays_out(s, kind):
+        sign = 1 - 2 * s
+        if kind:
+            return (x > 0) & (wrap(z - (2 * n_x - 2 * x) * sign) >= 8)
+        return wrap(z - 4 * sign) < 8
+
+    def relays_back(s, kind):
+        sign = 1 - 2 * s
+        if kind:
+            return (x < n_x - 1) & (wrap(z + (2 * x + 2) * sign) < 8)
+        return wrap(z + 4 * sign) >= 8
+
+    def start_out(c):
+        @pl.when(has_next)
+        def _():
+            for s in (0, 1):
+                leg0(c, s, out_kind).start()
+
+    def start_back(c):
+        @pl.when(has_previous)
+        def _():
+            for s in (0, 1):
+                leg2(c, s, back_kind).start()
+
+    def pass_on(relays, first, second, c):
         for s in (0, 1):
-            leg(c, s).start()
-
-    def arrive(leg, c):
-        for s in (0, 1):
-            leg(c, s).wait_recv()
-
-    def forward(first, second, c):
-        for s in (0, 1):
-            first(c, s).wait_recv()
-            second(c, s).start()
+            for kind in (0, 1):
+
+                @pl.when(relays(s, kind))
+                def _():
+                    first(c, s, kind).wait_recv()
+                    second(c, s, kind).start()
 
     for c in range(GROUP):
         for kind in (0, 1):
@@ -173,7 +217,7 @@
                 keep(kind).wait()
             else:
                 into(kind, c).wait_recv()
-        start(leg0, c)
+        start_out(c)
 
     for kind in (2, 3):
         keep(kind).start()
@@ -203,7 +247,7 @@
         dv_s[at, :] = jnp.zeros((TOK, HEAD), F32)
 
     def first_half(c, _):
-        forward(leg0, leg1, c)
+        pass_on(relays_out, leg0, leg1, c)
         table(block(c), c)
         table(block(c, SPAN), c + GROUP)
         hat(block(c, SPAN))
@@ -217,7 +261,16 @@
             into(kind, k).wait_recv()
 
     def previous_keys(c, _):
-        arrive(leg1, c)
+
+        @pl.when(has_previous)
+        def _():
+            for s in (0, 1):
+                leg1(c, s, 0).wait_recv()
+
+        @pl.when(g == 0)
+        def _():
+            land[block(chunk(c)), :] = jnp.zeros((TOK, 2 * HEAD), BF16)
+
         hat(block(chunk(c)))
         return 0
 
@@ -277,7 +330,7 @@
         dk_s[keys, :] += mm(ds, q, NN)
         ret_s[rows, :HEAD] = (dk_s[rows, :] * SCALE).astype(BF16)
         ret_s[rows, HEAD:] = dv_s[rows, :].astype(BF16)
-        start(leg2, b)
+        start_back(b)
         dq = (mm(kt_s[:, keys], ds, NN) * SCALE).T
         for h in range(2):
             back = prepare_back(raw[h], q_gain, cosine, sine, dq[h * TOK : (h + 1) * TOK, :])
@@ -285,18 +338,27 @@
 
         @pl.when(b >= 2)
         def _():
-            forward(leg2, leg3, b - 2)
+            pass_on(relays_back, leg2, leg3, b - 2)
 
         deliver(0, b)
         return 0
 
     lax.fori_loop(0, GROUP, step, 0)
     for c in (GROUP - 2, GROUP - 1):
-        forward(leg2, leg3, c)
+        pass_on(relays_back, leg2, leg3, c)
 
     def finish(b, _):
         rows, at = block(b), block(b, SPAN)
-        arrive(leg3, b)
+
+        @pl.when(has_next)
+        def _():
+            for s in (0, 1):
+                leg3(b, s, 0).wait_recv()
+
+        @pl.when(jnp.logical_not(has_next))
+        def _():
+            ret_l[rows, :] = jnp.zeros((TOK, 2 * HEAD), BF16)
+
         dk = dk_s[at, :] * SCALE + ret_l[rows, :HEAD].astype(F32)
         back = prepare_back(land[at, :HEAD].astype(F32), k_gain, cos_s[at, :], sin_s[at, :], dk)
         kvg_s[rows, :HEAD] = back.astype(BF16)
@@ -312,9 +374,26 @@
             into(kind, k).wait_send()
         share(k).wait_send()
     for c in range(GROUP):
-        for leg in (leg0, leg1, leg2, leg3):
-            for s in (0, 1):
-                leg(c, s).wait_send()
+        for s in (0, 1):
+
+            @pl.when(has_next)
+            def _():
+                leg0(c, s, out_kind).wait_send()
+
+            @pl.when(has_previous)
+            def _():
+                leg2(c, s, back_kind).wait_send()
+
+            for kind in (0, 1):
+
+                @pl.when(relays_out(s, kind))
+                def _():
+                    leg1(c, s, kind).wait_send()
+
+                @pl.when(relays_back(s, kind))
+                def _():
+                    leg3(c, s, kind).wait_send()
+
     for kind, result in ((0, oq), (1, ok), (2, ov)):
         for k in range(1, GROUP):
             p = lax.rem(r + k, GROUP)
@@ -362,8 +441,8 @@
             pltpu.VMEM((HEAD, 2 * SPAN), BF16),
             pltpu.VMEM((2 * SPAN, HEAD), F32),
             pltpu.VMEM((2 * SPAN, HEAD), F32),
-            pltpu.VMEM((SPAN, 2 * HEAD), BF16),
-            pltpu.VMEM((SPAN, 2 * HEAD), BF16),
+            pltpu.VMEM((2 * SPAN, 2 * HEAD), BF16),
+            pltpu.VMEM((2 * SPAN, 2 * HEAD), BF16),
             pltpu.VMEM((SPAN, 2 * HEAD), BF16),
             pltpu.VMEM((SPAN, 2 * HEAD), BF16),
             pltpu.VMEM((SPAN, 2 * HEAD), BF16),
@@ -372,7 +451,7 @@
             pltpu.VMEM((TOK, SPAN), BF16),
             pltpu.VMEM((TOK, SPAN), BF16),
             dma((4, 8)), dma((4, 8)), dma((8,)), dma((8,)),
-            dma((4, 2, 8)), dma((4, 2, 8)), dma((3, 8)), dma((3, 8)), dma((7,)),
+            dma((4, 2, 16)), dma((4, 2, 16)), dma((3, 8)), dma((3, 8)), dma((7,)),
         ],
         compiler_params=pltpu.CompilerParams(collective_id=0, has_side_effects=True),
         name="layer_backward",

time: 130 us -> 139 us (1.069)
  the two profiles are of different devices: /device:TPU:25 before, /device:TPU:93 now
where the time goes in v4:
time: 139 us; the launch traced here: 138 us
  Pallas kernels  135 us (97%)
    pallas_call x1, Pallas kernels, body(): pl.pallas_call(layer_kernel, out_shape=shapes, in_specs=[anywhere] * 4 +...  133 us

profile of v4, /device:TPU:93, one launch (start us, length us, event | category | flops | bytes accessed | tf_op | source)
XLA Modules:
  0.0 138.2 jit_solution(12760539258851935133)
XLA Ops:
  0.6 0.0 copy-start.3
  0.7 0.0 copy-start.4
  0.7 0.6 copy-done.3
  1.3 0.0 copy-done.4
  1.3 0.0 copy-start.1
  1.3 0.0 copy-start.2
  1.4 0.5 dynamic_update_slice.3.gain_in
  1.9 0.1 copy-done.1
  2.0 0.0 copy-done.2
  2.0 0.0 copy-start
  2.0 1.0 fusion
  3.0 0.0 copy-done
  3.0 133.0 %layer_backward.1 = (bf16[1,128,2048]{2,1,0:T(8,128)(2,1)}, bf16[1,128,1024]{2,1,0:T(8,128)(2,1)}, bf16[1,128,1024]{2,1,0:T(8,128)(2,1)}) custom-call(bf16[1,128,2048]{2,1,0:T(8,128)(2,1)} %q_in.1, bf16[1,128,1024]{2,1,0:T(8,128)(2,1)} %k_in.1, bf16[1,128,1024]{2,1,0:T(8,128)(2,1)} %v_in.1, bf16[1,128,2048]{2,1,0:T(8,128)(2,1)} %do_in.1, f32[8,128]{1,0:T(8,128)} %copy-done, ...), custom_call_target="tpu_custom_call" | custom-call | tf_op jit(solution)/shard_map/layer_backward/pallas_call | solution.py:429
  136.1 2.2 %settle.1 = (bf16[1,128,2048]{2,1,0:T(8,128)(2,1)}, bf16[1,128,1024]{2,1,0:T(8,128)(2,1)}, bf16[1,128,1024]{2,1,0:T(8,128)(2,1)}) custom-call(bf16[1,128,2048]{2,1,0:T(8,128)(2,1)} %get-tuple-element.6.a, bf16[1,128,1024]{2,1,0:T(8,128)(2,1)} %get-tuple-element.7.b, bf16[1,128,1024]{2,1,0:T(8,128)(2,1)} %get-tuple-element.8.c), custom_call_target="tpu_custom_call" | custom-call | tf_op jit(solution)/shard_map/settle/pallas_call | solution.py:462
  (3 shorter events, 0.0 us)
Async XLA Ops:
  0.6 0.7 copy-start.3
  0.7 0.7 copy-start.4
  1.3 0.7 copy-start.1
  1.3 0.7 copy-start.2
  2.0 1.0 copy-start

commit v5 on v3

--- a/solution.py
+++ b/solution.py
@@ -59,7 +59,7 @@
     q_in, k_in, v_in, do_in, gain_in, cos_in, sin_in,
     oq, ok, ov,
     land, qd, gain_s, cos_s, sin_s, k_s, kt_s, dk_s, dv_s,
-    relay_f, relay_b, ret_s, ret_l, qg_s, kvg_s, lq, lk, lv,
+    ret_s, ret_l, qg_s, kvg_s, lq, lk, lv,
     in_send, in_recv, gain_send, gain_recv, z_send, z_recv, out_send, out_recv, self_sem,
 ):
     d = lax.axis_index("dp")
@@ -75,12 +75,6 @@
     def mate(p):
         return (d, g * GROUP + p)
 
-    def place(px, pz):
-        return (lax.rem(pz, 8), (px * 2 + lax.div(pz, 8)) * GROUP + r)
-
-    def up(sign):
-        return lax.rem(z + 4 * sign + 16, 16)
-
     def remote(src, dst, send, recv, device):
         return pltpu.make_async_remote_copy(
             src_ref=src, dst_ref=dst, send_sem=send, recv_sem=recv, device_id=device, device_id_type=MESH
@@ -95,10 +89,11 @@
         greet(mate(lax.rem(r + k, GROUP)))
     for k in range(1, 8):
         greet((lax.rem(d + k, 8), seq))
-    for dx in (-1, 0, 1):
-        for hi in (0, 1):
-            greet((lax.rem(d + 4, 8), (lax.rem(x + dx + n_x, n_x) * 2 + hi) * GROUP + r))
-    pl.semaphore_wait(barrier, 20)
+    after = (d, lax.rem(g + 1, n_g) * GROUP + r)
+    before = (d, lax.rem(g + n_g - 1, n_g) * GROUP + r)
+    greet(after)
+    greet(before)
+    pl.semaphore_wait(barrier, 16)
 
     kinds = (
         (k_in, HEAD, land, SPAN, 0),
@@ -140,19 +135,10 @@
         return remote(src, dst, z_send.at[leg, s, c], z_recv.at[leg, s, c], device)
 
     def leg0(c, s):
-        return hop(0, c, s, land.at[half(chunk(c), s, SPAN), :], relay_f.at[half(c, s), :], place(x, up(1 - 2 * s)))
+        return hop(0, c, s, land.at[half(chunk(c), s, SPAN), :], land.at[half(chunk(c), s), :], after)
 
     def leg1(c, s):
-        sign = 1 - 2 * s
-        to = place(lax.rem(x + lax.div(up(-sign), 8), n_x), up(sign))
-        return hop(1, c, s, relay_f.at[half(c, s), :], land.at[half(chunk(c), s), :], to)
-
-    def leg2(c, s):
-        to = place(lax.rem(x + n_x - 1 + lax.div(z, 8), n_x), up(2 * s - 1))
-        return hop(2, c, s, ret_s.at[half(c, s), :], relay_b.at[half(c, s), :], to)
-
-    def leg3(c, s):
-        return hop(3, c, s, relay_b.at[half(c, s), :], ret_l.at[half(c, s), :], place(x, up(2 * s - 1)))
+        return hop(1, c, s, ret_s.at[half(c, s), :], ret_l.at[half(c, s), :], before)
 
     def start(leg, c):
         for s in (0, 1):
@@ -161,11 +147,6 @@
     def arrive(leg, c):
         for s in (0, 1):
             leg(c, s).wait_recv()
-
-    def forward(first, second, c):
-        for s in (0, 1):
-            first(c, s).wait_recv()
-            second(c, s).start()
 
     for c in range(GROUP):
         for kind in (0, 1):
@@ -203,7 +184,6 @@
         dv_s[at, :] = jnp.zeros((TOK, HEAD), F32)
 
     def first_half(c, _):
-        forward(leg0, leg1, c)
         table(block(c), c)
         table(block(c, SPAN), c + GROUP)
         hat(block(c, SPAN))
@@ -217,7 +197,7 @@
             into(kind, k).wait_recv()
 
     def previous_keys(c, _):
-        arrive(leg1, c)
+        arrive(leg0, c)
         hat(block(chunk(c)))
         return 0
 
@@ -277,26 +257,20 @@
         dk_s[keys, :] += mm(ds, q, NN)
         ret_s[rows, :HEAD] = (dk_s[rows, :] * SCALE).astype(BF16)
         ret_s[rows, HEAD:] = dv_s[rows, :].astype(BF16)
-        start(leg2, b)
+        start(leg1, b)
         dq = (mm(kt_s[:, keys], ds, NN) * SCALE).T
         for h in range(2):
             back = prepare_back(raw[h], q_gain, cosine, sine, dq[h * TOK : (h + 1) * TOK, :])
             qg_s[rows, h * HEAD : (h + 1) * HEAD] = back.astype(BF16)
 
-        @pl.when(b >= 2)
-        def _():
-            forward(leg2, leg3, b - 2)
-
         deliver(0, b)
         return 0
 
     lax.fori_loop(0, GROUP, step, 0)
-    for c in (GROUP - 2, GROUP - 1):
-        forward(leg2, leg3, c)
 
     def finish(b, _):
         rows, at = block(b), block(b, SPAN)
-        arrive(leg3, b)
+        arrive(leg1, b)
         dk = dk_s[at, :] * SCALE + ret_l[rows, :HEAD].astype(F32)
         back = prepare_back(land[at, :HEAD].astype(F32), k_gain, cos_s[at, :], sin_s[at, :], dk)
         kvg_s[rows, :HEAD] = back.astype(BF16)
@@ -312,7 +286,7 @@
             into(kind, k).wait_send()
         share(k).wait_send()
     for c in range(GROUP):
-        for leg in (leg0, leg1, leg2, leg3):
+        for leg in (leg0, leg1):
             for s in (0, 1):
                 leg(c, s).wait_send()
     for kind, result in ((0, oq), (1, ok), (2, ov)):
@@ -366,13 +340,11 @@
             pltpu.VMEM((SPAN, 2 * HEAD), BF16),
             pltpu.VMEM((SPAN, 2 * HEAD), BF16),
             pltpu.VMEM((SPAN, 2 * HEAD), BF16),
-            pltpu.VMEM((SPAN, 2 * HEAD), BF16),
-            pltpu.VMEM((SPAN, 2 * HEAD), BF16),
             pltpu.VMEM((TOK, 2 * SPAN), BF16),
             pltpu.VMEM((TOK, SPAN), BF16),
             pltpu.VMEM((TOK, SPAN), BF16),
             dma((4, 8)), dma((4, 8)), dma((8,)), dma((8,)),
-            dma((4, 2, 8)), dma((4, 2, 8)), dma((3, 8)), dma((3, 8)), dma((7,)),
+            dma((2, 2, 8)), dma((2, 2, 8)), dma((3, 8)), dma((3, 8)), dma((7,)),
         ],
         compiler_params=pltpu.CompilerParams(collective_id=0, has_side_effects=True),
         name="layer_backward",

time: 130 us -> 133 us (1.023)
  the two profiles are of different devices: /device:TPU:25 before, /device:TPU:507 now
where the time goes in v5:
time: 133 us
  Pallas kernels  130 us (98%)
    pallas_call x1, Pallas kernels, body(): pl.pallas_call(layer_kernel, out_shape=shapes, in_specs=[anywhere] * 4 +...  128 us

profile of v5, /device:TPU:507, one launch (start us, length us, event | category | flops | bytes accessed | tf_op | source)
XLA Modules:
  0.0 133.0 jit_solution(11292657680811799484)
XLA Ops:
  0.6 0.0 copy-start.3
  0.7 0.0 copy-start.4
  0.7 0.6 copy-done.3
  1.3 0.0 copy-done.4
  1.3 0.0 copy-start.1
  1.3 0.0 copy-start.2
  1.4 0.5 dynamic_update_slice.3.gain_in
  1.9 0.1 copy-done.1
  2.0 0.0 copy-done.2
  2.0 0.0 copy-start
  2.0 1.0 fusion
  3.0 0.0 copy-done
  3.0 127.8 %layer_backward.1 = (bf16[1,128,2048]{2,1,0:T(8,128)(2,1)}, bf16[1,128,1024]{2,1,0:T(8,128)(2,1)}, bf16[1,128,1024]{2,1,0:T(8,128)(2,1)}) custom-call(bf16[1,128,2048]{2,1,0:T(8,128)(2,1)} %q_in.1, bf16[1,128,1024]{2,1,0:T(8,128)(2,1)} %k_in.1, bf16[1,128,1024]{2,1,0:T(8,128)(2,1)} %v_in.1, bf16[1,128,2048]{2,1,0:T(8,128)(2,1)} %do_in.1, f32[8,128]{1,0:T(8,128)} %copy-done, ...), custom_call_target="tpu_custom_call" | custom-call | tf_op jit(solution)/shard_map/layer_backward/pallas_call | solution.py:324
  130.8 2.2 %settle.1 = (bf16[1,128,2048]{2,1,0:T(8,128)(2,1)}, bf16[1,128,1024]{2,1,0:T(8,128)(2,1)}, bf16[1,128,1024]{2,1,0:T(8,128)(2,1)}) custom-call(bf16[1,128,2048]{2,1,0:T(8,128)(2,1)} %get-tuple-element.6.a, bf16[1,128,1024]{2,1,0:T(8,128)(2,1)} %get-tuple-element.7.b, bf16[1,128,1024]{2,1,0:T(8,128)(2,1)} %get-tuple-element.8.c), custom_call_target="tpu_custom_call" | custom-call | tf_op jit(solution)/shard_map/settle/pallas_call | solution.py:355
  (3 shorter events, 0.0 us)
Async XLA Ops:
  0.6 0.7 copy-start.3
  0.7 0.7 copy-start.4
  1.3 0.7 copy-start.1
  1.3 0.7 copy-start.2
  2.0 1.0 copy-start
